TPU v7x, 128 devices: a whole 4x4x4 slice. The times are simulated.
128 devices in a mesh: row: 8 (over z_hi, y), col: 16 (over z_lo, x, core).
Axes of the slice: x: 4, y: 4, z: 4 (z_hi: 2, z_lo: 2; z = z_hi * 2 + z_lo), core: 2. Of those that a mesh axis runs over, the one named last changes fastest.
Arguments:
- features: bfloat16 [16, 2048, 4096], P(None, 'row', 'col'), may hold values from -6 to 6
- conv_weight: bfloat16 [3, 16, 3, 3], replicated, may hold values from -0.5 to 0.5
- bias: float32 [3], replicated, may hold values from -3 to 3
- inv_wavelength: float32 [3], replicated, may hold values from 12 to 18
- distance: float32 [1], replicated, may hold values from 16000 to 32000
Outputs:
- propagated: bfloat16 [3, 2, 2048, 4096], P(None, None, ('row', 'col'))
All inputs are finite; a program needn't handle non-finite values.
Results may differ from a plain program's by a relative error of at most 0.0025.
Values may be sent and summed in bfloat16 or wider, within the bound.
A program may use at most 128 MiB of HBM per device.

v0:
```python
import functools
import math

import jax
import jax.numpy as jnp
import numpy as np
from jax import lax
from jax.experimental import pallas as pl
from jax.experimental.pallas import tpu as pltpu
from jax.sharding import PartitionSpec as P

F32 = jnp.float32
BF16 = jnp.bfloat16
VMEM_LIMIT = 56 * 1024 * 1024


def split_np(table):
    hi = table.astype(np.float32).astype(jnp.bfloat16)
    lo = (table - hi.astype(np.float64)).astype(np.float32).astype(jnp.bfloat16)
    return np.stack([np.asarray(hi), np.asarray(lo)])


def rotation_np(theta):
    return np.array([[np.cos(theta), np.sin(theta)], [-np.sin(theta), np.cos(theta)]])


def tables():
    k2 = np.arange(256)
    b = np.arange(256)
    rot = rotation_np(2.0 * np.pi * ((k2[:, None] * b[None, :]) % 256) / 256.0)
    forward_y = rot.reshape(2, 2, 64, 4, 256).transpose(2, 0, 3, 1, 4).reshape(512, 512)
    inverse_y = forward_y.T
    j = np.arange(16)
    rot16 = rotation_np(2.0 * np.pi * ((j[:, None] * j[None, :]) % 16) / 16.0)
    back16 = np.stack([np.stack([rot16[0, 0], -rot16[0, 1]]), np.stack([-rot16[1, 0], rot16[1, 1]])])
    spread16 = np.einsum("pqjk,rs->pjrqks", back16, np.eye(16)).reshape(512, 512)
    lanes = np.einsum("pqab,cd->qcbpda", rot16, np.eye(8)).reshape(256, 256)
    lanes_back = np.einsum("pqab,cd->qcbpda", back16, np.eye(8)).reshape(256, 256)
    k1 = np.arange(16)
    angle = 2.0 * np.pi * ((k1[:, None] * b[None, :]) % 4096) / 4096.0
    twist_y = np.stack([np.cos(angle), -np.sin(angle)]).astype(np.float32)
    twist_back = np.stack([np.cos(angle.T), np.sin(angle.T)])
    twist_back = np.repeat(twist_back, 16, axis=2).astype(np.float32)
    p = np.arange(128).reshape(64, 2)
    r = np.arange(16)
    angle = 2.0 * np.pi * ((p[:, :, None] * r) % 2048) / 2048.0
    twist_x = np.stack([np.cos(angle), -np.sin(angle)])
    twist_x = np.broadcast_to(twist_x[:, :, :, None, None, :], (2, 64, 2, 4, 8, 16))
    twist_x = twist_x.reshape(2, 64, 8, 128).astype(np.float32)
    return {
        "forward_y": split_np(forward_y * 8.0),
        "inverse_y": split_np(inverse_y * 2.0**-10),
        "spread16": split_np(spread16),
        "lanes": split_np(lanes),
        "lanes_back": split_np(lanes_back * 2.0**-16),
        "twist_y": twist_y,
        "twist_back": twist_back,
        "twist_x": twist_x,
    }


def encode(x):
    x = x * jnp.abs(x)
    x = x * jnp.abs(x)
    x = x * jnp.abs(x)
    return x.astype(BF16)


def decode(y):
    y = y.astype(F32)
    root = jnp.sqrt(jnp.sqrt(jnp.sqrt(jnp.abs(y))))
    return jnp.where(y < 0.0, -root, root)


def split(x):
    hi = x.astype(BF16)
    return hi, (x - hi.astype(F32)).astype(BF16)


def cos_sin_quarters(u):
    n = jnp.round(u)
    f = u - n
    n = n.astype(jnp.int32)
    z = f * f
    s = f * (1.5707963267948966 + z * (-0.6459640975062462 + z * (0.07969262624616703 + z * (-0.004681754135318688 + z * 0.00016044118478735982))))
    c = 1.0 + z * (-1.2337005501361697 + z * (0.253669507901048 + z * (-0.020863480763352960 + z * (0.0009192602748394265 - z * 2.5202042373060605e-05))))
    swap = (n & 1) == 1
    cos = jnp.where(swap, s, c)
    sin = jnp.where(swap, c, s)
    cos = jnp.where(((n + 1) & 2) == 2, -cos, cos)
    sin = jnp.where((n & 2) == 2, -sin, sin)
    return cos, sin


def fft4(x, sign):
    (ar, ai), (br, bi), (cr, ci), (dr, di) = x
    sr, si, tr, ti = ar + cr, ai + ci, ar - cr, ai - ci
    ur, ui, vr, vi = br + dr, bi + di, br - dr, bi - di
    if sign < 0:
        vr, vi = vi, -vr
    else:
        vr, vi = -vi, vr
    return [(sr + ur, si + ui), (tr + vr, ti + vi), (sr - ur, si - ui), (tr - vr, ti - vi)]


def scaled(x, angle):
    turn = angle / (0.5 * math.pi)
    xr, xi = x
    if abs(turn - round(turn)) < 1e-9:
        case = int(round(turn)) % 4
        return [(xr, xi), (-xi, xr), (-xr, -xi), (xi, -xr)][case]
    c, s = math.cos(angle), math.sin(angle)
    eighth = turn * 2
    if abs(eighth - round(eighth)) < 1e-9:
        case = int(round(eighth)) % 8
        h = math.sqrt(0.5)
        if case == 1:
            return ((xr - xi) * h, (xr + xi) * h)
        if case == 3:
            return ((xr + xi) * -h, (xr - xi) * h)
        if case == 5:
            return ((xi - xr) * h, (xr + xi) * -h)
        return ((xr + xi) * h, (xi - xr) * h)
    return (xr * c - xi * s, xr * s + xi * c)


def fft8(x, sign):
    even = fft4(x[0::2], sign)
    odd = fft4(x[1::2], sign)
    odd = [scaled(v, sign * 2.0 * math.pi * k / 8) for k, v in enumerate(odd)]
    first = [(a[0] + b[0], a[1] + b[1]) for a, b in zip(even, odd)]
    return first + [(a[0] - b[0], a[1] - b[1]) for a, b in zip(even, odd)]


def fft16(x, sign):
    inner = [fft4([x[4 * n1 + n2] for n1 in range(4)], sign) for n2 in range(4)]
    out = [None] * 16
    for k1 in range(4):
        column = [scaled(inner[n2][k1], sign * 2.0 * math.pi * n2 * k1 / 16) for n2 in range(4)]
        for k2, v in enumerate(fft4(column, sign)):
            out[k1 + 4 * k2] = v
    return out


def dot3(lhs, rhs, dims):
    one = functools.partial(lax.dot_general, dimension_numbers=(dims, ((), ())), preferred_element_type=F32)
    return one(lhs[0], rhs[0]) + (one(lhs[0], rhs[1]) + one(lhs[1], rhs[0]))


NN = ((1,), (0,))
NT = ((1,), (1,))


def rows_forward_kernel(phase_ref, matrix_ref, twist_ref, out_ref, hi_ref, lo_ref):
    for half in range(2):
        cols = pl.ds(half * 128, 128)
        field = []
        for j in range(16):
            field.append(cos_sin_quarters(2.0 * decode(phase_ref[j, :, cols])))
        spectrum = fft16(field, -1.0)
        for k1 in range(16):
            re, im = spectrum[k1]
            if k1 > 0:
                c = twist_ref[0, pl.ds(k1, 1), cols]
                s = twist_ref[1, pl.ds(k1, 1), cols]
                re, im = re * c - im * s, re * s + im * c
            rows = pl.ds(k1 * 16, 16)
            for part, value in enumerate((re, im)):
                hi, lo = split(value)
                place = pl.ds(part * 256 + half * 128, 128)
                hi_ref[rows, place] = hi
                lo_ref[rows, place] = lo
    result = dot3((matrix_ref[0], matrix_ref[1]), (hi_ref[...], lo_ref[...]), NT)
    for h in range(2):
        out_ref[:, h] = encode(result[:, h * 128 : (h + 1) * 128]).reshape(64, 8, 128)


def columns_kernel(wave_ref, travel_ref, in_ref, matrix_ref, back_ref, twist_ref, out_ref, re_ref, im_ref, hi_ref, lo_ref):
    color = pl.program_id(0)
    position = lax.axis_index("row") * 16 + lax.axis_index("col")
    row = lax.broadcasted_iota(jnp.int32, (8, 128), 0)
    lane = lax.broadcasted_iota(jnp.int32, (8, 128), 1)
    top = row < 4

    def tile(ref, k):
        return ref[k, 0]

    for n2 in range(8):
        column = []
        for n1 in range(8):
            s = 8 * n1 + n2
            a, b = decode(tile(in_ref, s)), decode(tile(in_ref, s + 64))
            total, delta = a + b, a - b
            re = jnp.where(top, total, pltpu.roll(delta, 4, 0))
            im = jnp.where(top, pltpu.roll(total, 4, 0), delta)
            if s > 0:
                angle = 2.0 * math.pi * s / 128
                c = jnp.where(top, 1.0, math.cos(angle))
                w = jnp.where(top, 0.0, math.sin(angle))
                re, im = re * c + im * w, im * c - re * w
            column.append((re, im))
        for m1, v in enumerate(fft8(column, -1.0)):
            re, im = scaled(v, -2.0 * math.pi * n2 * m1 / 64)
            re_ref[m1 * 8 + n2] = re
            im_ref[m1 * 8 + n2] = im
    for m1 in range(8):
        column = [(re_ref[m1 * 8 + n2], im_ref[m1 * 8 + n2]) for n2 in range(8)]
        points = fft8(column, -1.0)
        for pair in range(0, 8, 1):
            place = m1 + 8 * pair
            re, im = points[pair]
            c, w = twist_ref[0, place], twist_ref[1, place]
            re, im = re * c - im * w, re * w + im * c
            hi_re, lo_re = split(re)
            hi_im, lo_im = split(im)
            hi_ref[place, :, :128] = hi_re
            hi_ref[place, :, 128:] = hi_im
            lo_ref[place, :, :128] = lo_re
            lo_ref[place, :, 128:] = lo_im
    data = (hi_ref[...].reshape(512, 256), lo_ref[...].reshape(512, 256))
    spectrum = dot3(data, (matrix_ref[0], matrix_ref[1]), NN).reshape(64, 8, 256)
    wave = wave_ref[color]
    travel = travel_ref[0]
    base_x = (row // 4) + 128 * (lane % 16)
    freq_y = 8 * (position % 2) + lane // 16 + 16 * (4 * (position // 2) + row % 4)
    signed_y = jnp.where(freq_y < 2048, freq_y, freq_y - 4096).astype(F32) * (1.0 / 4096)
    square_y = signed_y * signed_y
    for place in range(64):
        freq_x = base_x + 2 * place
        signed_x = jnp.where(freq_x < 1024, freq_x, freq_x - 2048).astype(F32) * (1.0 / 2048)
        squared = signed_x * signed_x + square_y
        turns = travel * squared / (wave + jnp.sqrt(wave * wave - squared))
        c, w = cos_sin_quarters(4.0 * turns)
        re, im = spectrum[place, :, :128], spectrum[place, :, 128:]
        re, im = re * c + im * w, im * c - re * w
        hi_re, lo_re = split(re)
        hi_im, lo_im = split(im)
        hi_ref[place, :, :128] = hi_re
        hi_ref[place, :, 128:] = hi_im
        lo_ref[place, :, :128] = lo_re
        lo_ref[place, :, 128:] = lo_im
    data = (hi_ref[...].reshape(512, 256), lo_ref[...].reshape(512, 256))
    spectrum = dot3(data, (back_ref[0], back_ref[1]), NN).reshape(64, 8, 256)
    for m1 in range(8):
        column = []
        for m2 in range(8):
            place = m1 + 8 * m2
            re, im = spectrum[place, :, :128], spectrum[place, :, 128:]
            c, w = twist_ref[0, place], twist_ref[1, place]
            column.append((re * c + im * w, im * c - re * w))
        for n2, v in enumerate(fft8(column, 1.0)):
            re, im = scaled(v, 2.0 * math.pi * n2 * m1 / 64)
            re_ref[m1 * 8 + n2] = re
            im_ref[m1 * 8 + n2] = im
    for n2 in range(8):
        column = [(re_ref[m1 * 8 + n2], im_ref[m1 * 8 + n2]) for m1 in range(8)]
        for n1, (re, im) in enumerate(fft8(column, 1.0)):
            s = 8 * n1 + n2
            if s > 0:
                angle = 2.0 * math.pi * s / 128
                c = jnp.where(top, 1.0, math.cos(angle))
                w = jnp.where(top, 0.0, math.sin(angle))
                re, im = re * c - im * w, im * c + re * w
            total = jnp.where(top, re, pltpu.roll(im, 4, 0))
            delta = jnp.where(top, pltpu.roll(re, 4, 0), im)
            out_ref[s, 0] = encode(total + delta)
            out_ref[s + 64, 0] = encode(total - delta)


def rows_inverse_kernel(in_ref, matrix_ref, twist_ref, spread_ref, out_ref):
    left = decode(in_ref[:, 0]).reshape(512, 128)
    right = decode(in_ref[:, 1]).reshape(512, 128)
    data = split(jnp.concatenate([left, right], axis=1))
    value = dot3((matrix_ref[0], matrix_ref[1]), data, NN)
    re, im = value[:256], value[256:]
    c, s = twist_ref[0], twist_ref[1]
    value = jnp.concatenate([re * c - im * s, re * s + im * c], axis=1)
    result = dot3((spread_ref[0], spread_ref[1]), split(value), NT)
    for part in range(2):
        for j in range(16):
            rows = result[part * 256 + j * 16 : part * 256 + j * 16 + 16, :]
            out_ref[part, :, j * 256 : (j + 1) * 256] = rows.astype(BF16)


def whole(array):
    return pl.BlockSpec(array.shape, lambda o: (0,) * array.ndim, pipeline_mode=pl.Buffered(1))


def params():
    return pltpu.CompilerParams(dimension_semantics=("arbitrary",), vmem_limit_bytes=VMEM_LIMIT)


def rows_forward(phase, table):
    colors = phase.shape[1]
    args = (jnp.asarray(table["forward_y"]), jnp.asarray(table["twist_y"]))
    return pl.pallas_call(
        rows_forward_kernel,
        grid=(colors,),
        in_specs=[pl.BlockSpec((16, None, 16, 256), lambda o: (0, o, 0, 0)), whole(args[0]), whole(args[1])],
        out_specs=pl.BlockSpec((64, 2, None, 8, 128), lambda o: (0, 0, o, 0, 0)),
        out_shape=jax.ShapeDtypeStruct((64, 2, colors, 8, 128), BF16),
        scratch_shapes=[pltpu.VMEM((256, 512), BF16), pltpu.VMEM((256, 512), BF16)],
        compiler_params=params(),
        name="rows_forward",
    )(phase, *args)


def columns(spread, wave, travel, table):
    colors = spread.shape[1]
    args = tuple(jnp.asarray(table[k]) for k in ("lanes", "lanes_back", "twist_x"))
    block = pl.BlockSpec((128, 1, 8, 128), lambda o: (0, o, 0, 0))
    smem = pl.BlockSpec(memory_space=pltpu.SMEM)
    return pl.pallas_call(
        columns_kernel,
        grid=(colors,),
        in_specs=[smem, smem, block] + [whole(a) for a in args],
        out_specs=block,
        out_shape=jax.ShapeDtypeStruct((128, colors, 8, 128), BF16),
        scratch_shapes=[
            pltpu.VMEM((64, 8, 128), F32),
            pltpu.VMEM((64, 8, 128), F32),
            pltpu.VMEM((64, 8, 256), BF16),
            pltpu.VMEM((64, 8, 256), BF16),
        ],
        compiler_params=params(),
        name="columns",
    )(wave, travel, spread, *args)


def rows_inverse(returned, table):
    colors = returned.shape[2]
    args = tuple(jnp.asarray(table[k]) for k in ("inverse_y", "twist_back", "spread16"))
    return pl.pallas_call(
        rows_inverse_kernel,
        grid=(colors,),
        in_specs=[pl.BlockSpec((64, 2, None, 8, 128), lambda o: (0, 0, o, 0, 0))] + [whole(a) for a in args],
        out_specs=pl.BlockSpec((None, 2, 16, 4096), lambda o: (o, 0, 0, 0)),
        out_shape=jax.ShapeDtypeStruct((colors, 2, 16, 4096), BF16),
        compiler_params=params(),
        name="rows_inverse",
    )(returned, *args)


def extended(x, sides, width):
    for axis, dim in sides:
        peers, length = (lax.axis_size(axis), x.shape[dim])
        up = [(i, (i + 1) % peers) for i in range(peers - 1)]
        down = [(j, i) for i, j in up]
        last = lax.slice_in_dim(x, length - width, length, axis=dim)
        first = lax.slice_in_dim(x, 0, width, axis=dim)
        before = lax.ppermute(last, axis, up)
        after = lax.ppermute(first, axis, down)
        x = jnp.concatenate([before, x, after], axis=dim)
    return x


def head_conv(padded, conv_weight, tile_rows, tile_cols):
    score = jnp.zeros((conv_weight.shape[0], tile_rows, tile_cols), jnp.float32)
    for shift_u in range(3):
        for shift_v in range(3):
            window = padded[:, shift_u : shift_u + tile_rows, shift_v : shift_v + tile_cols]
            score = score + jnp.einsum(
                "oc,cxy->oxy",
                conv_weight[:, :, shift_u, shift_v],
                window,
                preferred_element_type=jnp.float32,
            )
    return score


def per_device(features, conv_weight, bias, inv_wavelength, distance):
    table = tables()
    tile_rows, tile_cols = features.shape[1:]
    padded = extended(features, (("row", 1), ("col", 2)), 1)
    score = head_conv(padded, conv_weight, tile_rows, tile_cols)
    coded = encode(jnp.tanh(score + bias[:, None, None]))
    coded = coded.reshape(3, 16, 16, 256).transpose(1, 0, 2, 3)
    pencils = lax.all_to_all(coded, "col", split_axis=0, concat_axis=0, tiled=True)
    packets = rows_forward(pencils, table).reshape(128, 3, 8, 128)
    spread = lax.all_to_all(packets, ("row", "col"), split_axis=0, concat_axis=0, tiled=True)
    packets = columns(spread, inv_wavelength, distance, table)
    returned = lax.all_to_all(packets, ("row", "col"), split_axis=0, concat_axis=0, tiled=True)
    return rows_inverse(returned.reshape(64, 2, 3, 8, 128), table)


def solution(mesh):
    in_specs = (P(None, "row", "col"), P(), P(), P(), P())
    out_specs = P(None, None, ("row", "col"), None)
    return jax.shard_map(
        per_device, mesh=mesh, in_specs=in_specs, out_specs=out_specs, check_vma=False
    )
```

profile of v0, /device:TPU:1, one launch (start us, length us, event | category | flops | bytes accessed | tf_op | source)
XLA Modules:
  0.0 132.2 jit_solution(2824580073866209699)
XLA Ops:
  0.0 0.0 copy-start
  0.0 0.0 copy-start.10
  0.0 2.9 %copy.40 = bf16[16,256,256]{2,0,1:T(8,128)(2,1)S(1)} copy(bf16[16,256,256]{2,1,0:T(8,128)(2,1)} %param.13) | data formatting | bytes 4194304 | tf_op args[0]
  2.9 0.0 copy-start.4
  3.0 4.0 %collective-permute-start = (bf16[16,1,256]{2,0,1:T(8,128)(2,1)S(1)}, bf16[16,1,256]{2,0,1:T(8,128)(2,1)S(1)}, u32[]{:S(2)}, u32[]{:S(2)}) collective-permute-start(bf16[16,1,256]{2,0,1:T(8,128)(2,1)S(1)} %get-tuple-element.8), channel_id=1, source_target_pairs={{0,16},{16,32},{32,48},{48,64},{64,80},{80,96},{96,112},{1,17},{17... | collective-permute-start | bytes 24584 | tf_op jit(solution)/shard_map/ppermute | solution.py:351
  7.0 1.3 collective-permute-start.1
  8.3 0.0 copy-done.10
  8.3 0.0 copy-done
  8.3 2.3 %fusion.35 = f32[3,256,256]{2,0,1:T(4,128)} fusion(bf16[3,16,1,1]{1,3,2,0:T(2,128)(2,1)S(1)} %get-tuple-element.12, bf16[16,256,256]{2,1,0:T(8,128)(2,1)S(1)} %copy-done), kind=kOutput, calls=%fused_computation.56 | convolution fusion | flops 6291456 | bytes 2883680 | tf_op jit(solution)/shard_map/oc,cxy->oxy/dot_general | solution.py:362
  10.6 0.0 collective-permute-done
  10.6 1.2 constant_dynamic-update-slice_fusion.1
  11.8 0.0 copy-done.4
  11.8 0.0 collective-permute-done.1
  11.9 1.5 %fusion.55 = (bf16[16,258,1]{2,0,1:T(8,128)(2,1)}, bf16[16,258,1]{2,0,1:T(8,128)(2,1)S(1)}) fusion(bf16[16,258,256]{2,0,1:T(8,128)(2,1)S(1)} %constant_dynamic-update-slice_fusion), kind=kLoop, calls=%fused_computation.76 | loop fusion | bytes 33024 | tf_op jit(solution)/shard_map/slice | solution.py:349
  13.3 2.1 %copy.43 = bf16[16,258,1]{1,0,2:T(8,128)(2,1)S(1)} copy(bf16[16,258,1]{2,0,1:T(8,128)(2,1)} %get-tuple-element.5) | data formatting | bytes 16512 | tf_op jit(solution)/shard_map/slice | solution.py:349
  15.5 4.6 %collective-permute-start.2 = (bf16[16,258,1]{1,0,2:T(8,128)(2,1)S(1)}, bf16[16,258,1]{1,0,2:T(8,128)(2,1)S(1)}, u32[]{:S(2)}, u32[]{:S(2)}) collective-permute-start(bf16[16,258,1]{1,0,2:T(8,128)(2,1)S(1)} %copy.43), channel_id=1, source_target_pairs={{0,1},{1,2},{2,3},{3,4},{4,5},{5,6},{6,7},{7,8},{8,9},{9,10},{10,1... | collective-permute-start | bytes 24776 | tf_op jit(solution)/shard_map/ppermute | solution.py:351
  20.1 1.1 copy.48
  21.2 0.0 copy-start.5
  21.2 2.2 %collective-permute-start.3 = (bf16[16,258,1]{1,0,2:T(8,128)(2,1)S(1)}, bf16[16,258,1]{1,0,2:T(8,128)(2,1)S(1)}, u32[]{:S(2)}, u32[]{:S(2)}) collective-permute-start(bf16[16,258,1]{1,0,2:T(8,128)(2,1)S(1)} %copy.48), channel_id=1, source_target_pairs={{1,0},{2,1},{3,2},{4,3},{5,4},{6,5},{7,6},{8,7},{9,8},{10,9},{11,1... | collective-permute-start | bytes 24776 | tf_op jit(solution)/shard_map/ppermute | solution.py:352
  23.4 3.0 %fusion = f32[256,256,3]{1,2,0:T(4,128)} fusion(bf16[16,256,256]{2,0,1:T(8,128)(2,1)} %copy-done.4, bf16[16,1,256]{2,0,1:T(8,128)(2,1)S(1)} %collective-permute-done, bf16[3,16,1,1]{1,3,2,0:T(2,128)(2,1)S(1)} %get-tuple-element.15), kind=kOutput, calls=%fused_computation.8 | convolution fusion | flops 10502144 | bytes 2891872 | tf_op jit(solution)/shard_map/oc,cxy->oxy/dot_general | solution.py:362
  26.4 0.0 copy-done.5
  26.4 1.4 %fusion.4 = f32[256,256,3]{1,2,0:T(4,128)} fusion(bf16[16,1,256]{2,0,1:T(8,128)(2,1)S(1)} %collective-permute-done.1, bf16[16,256,256]{2,0,1:T(8,128)(2,1)S(1)} %copy-done.5, bf16[3,16,1,1]{1,3,2,0:T(2,128)(2,1)S(1)} %get-tuple-element.17), kind=kOutput, calls=%fused_computation.12 | convolution fusion | flops 10502144 | bytes 2891872 | tf_op jit(solution)/shard_map/oc,cxy->oxy/dot_general | solution.py:362
  27.8 0.0 collective-permute-done.2
  27.8 1.2 copy.44
  29.0 2.0 %fusion.16 = f32[256,256,3]{1,2,0:T(4,128)} fusion(bf16[16,258,256]{2,0,1:T(8,128)(2,1)S(1)} %constant_dynamic-update-slice_fusion, bf16[16,258,1]{2,0,1:T(8,128)(2,1)S(1)} %copy.44, bf16[3,16,1,1]{1,3,2,0:T(2,128)(2,1)S(1)} %get-tuple-element.9), kind=kOutput, calls=%fused_computation.26 | convolution fusion | flops 10485760 | bytes 2908320 | tf_op jit(solution)/shard_map/oc,cxy->oxy/dot_general | solution.py:362
  31.0 2.0 %fusion.18 = f32[256,256,3]{1,2,0:T(4,128)} fusion(bf16[16,258,256]{2,0,1:T(8,128)(2,1)S(1)} %constant_dynamic-update-slice_fusion, bf16[16,258,1]{2,0,1:T(8,128)(2,1)S(1)} %copy.44, bf16[3,16,1,1]{1,3,2,0:T(2,128)(2,1)S(1)} %get-tuple-element.13), kind=kOutput, calls=%fused_computation.27 | convolution fusion | flops 10485760 | bytes 2908320 | tf_op jit(solution)/shard_map/oc,cxy->oxy/dot_general | solution.py:362
  32.9 0.0 collective-permute-done.3
  32.9 2.1 %copy.49 = bf16[16,258,1]{2,0,1:T(8,128)(2,1)} copy(bf16[16,258,1]{1,0,2:T(8,128)(2,1)S(1)} %collective-permute-done.3) | data formatting | bytes 16512 | tf_op jit(solution)/shard_map/ppermute | solution.py:352
  35.0 0.0 copy-start.1
  35.0 2.5 %fusion.20 = f32[256,256,3]{1,2,0:T(4,128)S(1)} fusion(bf16[16,258,256]{2,0,1:T(8,128)(2,1)S(1)} %constant_dynamic-update-slice_fusion, bf16[16,258,1]{2,0,1:T(8,128)(2,1)} %copy.49, bf16[3,16,1,1]{1,3,2,0:T(2,128)(2,1)S(1)} %get-tuple-element.14), kind=kOutput, calls=%fused_computation.28 | convolution fusion | flops 10485760 | bytes 2908320 | tf_op jit(solution)/shard_map/oc,cxy->oxy/dot_general | solution.py:362
  37.5 0.0 copy-done.1
  37.5 1.2 fusion.22
  38.7 0.0 copy-start.9
  38.7 1.0 fusion.14
  39.6 0.0 copy-start.2
  39.7 0.0 copy-start.6
  39.7 0.0 copy-start.7
  39.7 0.0 copy-start.8
  39.7 0.0 copy-start.11
  39.7 1.1 fusion.12
  40.8 0.0 copy-done.9
  40.8 0.1 copy-done.2
  40.9 0.3 copy-done.6
  41.3 0.3 copy-done.7
  41.6 0.3 copy-done.8
  41.9 0.0 copy-done.11
  41.9 1.2 fusion.24
  43.1 14.5 %all_to_all.15.phase_ref = bf16[16,3,16,256]{3,2,1,0:T(8,128)(2,1)} all-to-all(bf16[16,3,16,256]{3,2,1,0:T(8,128)(2,1)S(1)} %bitcast.60), channel_id=1, replica_groups=mesh['row'=8,'col'=16] {'col'}, dimensions={0} | all-to-all | bytes 786432 | tf_op jit(solution)/shard_map/all_to_all | solution.py:378
  57.6 6.2 %rows_forward.1 = bf16[64,2,3,8,128]{4,3,2,1,0:T(8,128)(2,1)} custom-call(bf16[16,3,16,256]{3,2,1,0:T(8,128)(2,1)} %all_to_all.15.phase_ref, bf16[2,512,512]{2,1,0:T(8,128)(2,1)} %constant.16.clone.matrix_ref, f32[2,16,256]{2,1,0:T(8,128)} %constant.17.clone.twist_ref), custom_call_target="tpu_custom_call" | custom-call | tf_op jit(solution)/shard_map/rows_forward/pallas_call | solution.py:296
  63.8 10.3 %all-to-all-start.1 = ((bf16[128,3,8,128]{3,2,1,0:T(8,128)(2,1)}), bf16[128,3,8,128]{3,2,1,0:T(8,128)(2,1)S(1)}, u32[]{:S(2)}, u32[]{:S(2)}) async-start(bf16[128,3,8,128]{3,2,1,0:T(8,128)(2,1)} %bitcast.58), calls=%async_computation.1 | async-start | bytes 1572864 | tf_op jit(solution)/shard_map/all_to_all | solution.py:380
  74.7 16.2 %all-to-all-done.1.in_ref = bf16[128,3,8,128]{3,2,1,0:T(8,128)(2,1)S(1)} async-done(((bf16[128,3,8,128]{3,2,1,0:T(8,128)(2,1)}), bf16[128,3,8,128]{3,2,1,0:T(8,128)(2,1)S(1)}, u32[]{:S(2)}, u32[]{:S(2)}) %all-to-all-start.1) | async-done | bytes 786464 | tf_op jit(solution)/shard_map/all_to_all | solution.py:380
  90.9 0.0 copy-start.3
  90.9 0.9 copy-done.3
  91.8 9.4 %columns.1 = bf16[128,3,8,128]{3,2,1,0:T(8,128)(2,1)} custom-call(f32[3]{0:T(128)} %wave_ref.1, f32[1]{0:T(128)S(6)} %copy.127.travel_ref, bf16[128,3,8,128]{3,2,1,0:T(8,128)(2,1)} %copy-done.3, bf16[2,256,256]{2,1,0:T(8,128)(2,1)} %constant.18.clone.matrix_ref, bf16[2,256,256]{2,1,0:T(8,128)(2,1)} %constant.19.clone.back_ref, ...), custom_call_target="tpu_custom_call" | custom-call | tf_op jit(solution)/shard_map/columns/pallas_call | solution.py:313
  101.2 21.9 %all_to_all.16 = bf16[128,3,8,128]{3,2,1,0:T(8,128)(2,1)} all-to-all(bf16[128,3,8,128]{3,2,1,0:T(8,128)(2,1)} %columns.1), channel_id=1, replica_groups=mesh['row'=8,'col'=16] {'row','col'}, dimensions={0} | all-to-all | bytes 1572864 | tf_op jit(solution)/shard_map/all_to_all | solution.py:382
  123.1 9.1 %rows_inverse.1 = bf16[3,2,16,4096]{3,2,1,0:T(8,128)(2,1)} custom-call(bf16[64,2,3,8,128]{4,3,2,1,0:T(8,128)(2,1)} %bitcast.57, bf16[2,512,512]{2,1,0:T(8,128)(2,1)} %constant.21.clone.matrix_ref, f32[2,256,256]{2,1,0:T(8,128)} %constant.22.clone.twist_ref, bf16[2,512,512]{2,1,0:T(8,128)(2,1)} %constant.23.clone.spread_ref), custom_call_target="tpu_custom_call" | custom-call | tf_op jit(solution)/shard_map/rows_inverse/pallas_call | solution.py:333
  (5 shorter events, 0.1 us)
Async XLA Ops:
  0.0 8.3 %copy-start = (bf16[16,256,256]{2,1,0:T(8,128)(2,1)S(1)}, bf16[16,256,256]{2,1,0:T(8,128)(2,1)}, u32[]{:S(2)}) copy-start(bf16[16,256,256]{2,1,0:T(8,128)(2,1)} %param.13) | copy-start | bytes 6291460
  0.0 8.3 %copy-start.10 = (bf16[3,16,3,3]{1,3,2,0:T(4,128)(2,1)S(1)}, bf16[3,16,3,3]{1,3,2,0:T(4,128)(2,1)}, u32[]{:S(2)}) copy-start(bf16[3,16,3,3]{1,3,2,0:T(4,128)(2,1)} %param.14) | copy-start | bytes 2596
  2.9 8.9 %copy-start.4 = (bf16[16,256,256]{2,0,1:T(8,128)(2,1)}, bf16[16,256,256]{2,0,1:T(8,128)(2,1)S(1)}, u32[]{:S(2)}) copy-start(bf16[16,256,256]{2,0,1:T(8,128)(2,1)S(1)} %copy.40) | copy-start | bytes 6291460
  3.0 7.7 %collective-permute-start = (bf16[16,1,256]{2,0,1:T(8,128)(2,1)S(1)}, bf16[16,1,256]{2,0,1:T(8,128)(2,1)S(1)}, u32[]{:S(2)}, u32[]{:S(2)}) collective-permute-start(bf16[16,1,256]{2,0,1:T(8,128)(2,1)S(1)} %get-tuple-element.8), channel_id=1, source_target_pairs={{0,16},{16,32},{32,48},{48,64},{64,80},{80,96},{96,112},{1,17},{17... | collective-permute-start | bytes 24584 | tf_op jit(solution)/shard_map/ppermute | solution.py:351
  7.0 4.8 %collective-permute-start.1 = (bf16[16,1,256]{2,0,1:T(8,128)(2,1)S(1)}, bf16[16,1,256]{2,0,1:T(8,128)(2,1)S(1)}, u32[]{:S(2)}, u32[]{:S(2)}) collective-permute-start(bf16[16,1,256]{2,0,1:T(8,128)(2,1)S(1)} %get-tuple-element.7), channel_id=1, source_target_pairs={{16,0},{32,16},{48,32},{64,48},{80,64},{96,80},{112,96},{17,1},{33... | collective-permute-start | bytes 24584 | tf_op jit(solution)/shard_map/ppermute | solution.py:352
  15.5 12.3 %collective-permute-start.2 = (bf16[16,258,1]{1,0,2:T(8,128)(2,1)S(1)}, bf16[16,258,1]{1,0,2:T(8,128)(2,1)S(1)}, u32[]{:S(2)}, u32[]{:S(2)}) collective-permute-start(bf16[16,258,1]{1,0,2:T(8,128)(2,1)S(1)} %copy.43), channel_id=1, source_target_pairs={{0,1},{1,2},{2,3},{3,4},{4,5},{5,6},{6,7},{7,8},{8,9},{9,10},{10,1... | collective-permute-start | bytes 24776 | tf_op jit(solution)/shard_map/ppermute | solution.py:351
  21.2 5.2 %copy-start.5 = (bf16[16,256,256]{2,0,1:T(8,128)(2,1)S(1)}, bf16[16,256,256]{2,0,1:T(8,128)(2,1)}, u32[]{:S(2)}) copy-start(bf16[16,256,256]{2,0,1:T(8,128)(2,1)} %copy-done.4) | copy-start | bytes 6291460
  21.2 11.7 %collective-permute-start.3 = (bf16[16,258,1]{1,0,2:T(8,128)(2,1)S(1)}, bf16[16,258,1]{1,0,2:T(8,128)(2,1)S(1)}, u32[]{:S(2)}, u32[]{:S(2)}) collective-permute-start(bf16[16,258,1]{1,0,2:T(8,128)(2,1)S(1)} %copy.48), channel_id=1, source_target_pairs={{1,0},{2,1},{3,2},{4,3},{5,4},{6,5},{7,6},{8,7},{9,8},{10,9},{11,1... | collective-permute-start | bytes 24776 | tf_op jit(solution)/shard_map/ppermute | solution.py:352
  35.0 2.5 %copy-start.1 = (bf16[16,258,1]{2,0,1:T(8,128)(2,1)S(1)}, bf16[16,258,1]{2,0,1:T(8,128)(2,1)}, u32[]{:S(2)}) copy-start(bf16[16,258,1]{2,0,1:T(8,128)(2,1)} %copy.49) | copy-start | bytes 24772
  38.7 2.2 %copy-start.9 = (f32[256,256,3]{1,2,0:T(4,128)S(1)}, f32[256,256,3]{1,2,0:T(4,128)}, u32[]{:S(2)}) copy-start(f32[256,256,3]{1,2,0:T(4,128)} %fusion.18) | copy-start | bytes 2359300
  39.6 1.3 copy-start.2
  39.7 1.6 %copy-start.6 = (f32[256,256,3]{1,2,0:T(4,128)S(1)}, f32[256,256,3]{1,2,0:T(4,128)}, u32[]{:S(2)}) copy-start(f32[256,256,3]{1,2,0:T(4,128)} %fusion) | copy-start | bytes 2359300
  39.7 1.9 %copy-start.7 = (f32[256,256,3]{1,2,0:T(4,128)S(1)}, f32[256,256,3]{1,2,0:T(4,128)}, u32[]{:S(2)}) copy-start(f32[256,256,3]{1,2,0:T(4,128)} %fusion.4) | copy-start | bytes 2359300
  39.7 2.2 %copy-start.8 = (f32[256,256,3]{1,2,0:T(4,128)S(1)}, f32[256,256,3]{1,2,0:T(4,128)}, u32[]{:S(2)}) copy-start(f32[256,256,3]{1,2,0:T(4,128)} %fusion.16) | copy-start | bytes 2359300
  39.7 2.2 %copy-start.11 = (f32[3]{0:T(128)S(1)}, f32[3]{0:T(128)}, u32[]{:S(2)}) copy-start(f32[3]{0:T(128)} %param.15) | copy-start | bytes 40
  63.8 27.1 %all-to-all-start.1 = ((bf16[128,3,8,128]{3,2,1,0:T(8,128)(2,1)}), bf16[128,3,8,128]{3,2,1,0:T(8,128)(2,1)S(1)}, u32[]{:S(2)}, u32[]{:S(2)}) async-start(bf16[128,3,8,128]{3,2,1,0:T(8,128)(2,1)} %bitcast.58), calls=%async_computation.1 | async-start | bytes 1572864 | tf_op jit(solution)/shard_map/all_to_all | solution.py:380
  90.9 0.9 copy-start.3
where the time goes:
time: 133 us; the launch traced here: 132 us
  blocking collectives  36.4 us (27%)
  Pallas kernels  24.7 us (19%)
  starting transfers between devices  22.4 us (17%)
  matrix products  16.4 us (12%)
  waiting for transfers between devices  16.2 us (12%)
  local copies, waits for them, and re-layouts  14.1 us (11%)
    all_to_all x1, blocking collectives, per_device(): lax.all_to_all(packets, ('row', 'col'), split_axis=0, concat_axis=0, tile...  21.9 us
    dot_general x9, matrix products, head_conv(): jnp.einsum('oc,cxy->oxy', conv_weight[:, :, shift_u, shift_v], window, pr...  16.4 us
    all_to_all x1, waiting for transfers between devices, per_device(): lax.all_to_all(packets, ('row', 'col'), split_axis=0, concat_axis=0, tile...  16.2 us
    all_to_all x1, blocking collectives, per_device(): lax.all_to_all(coded, 'col', split_axis=0, concat_axis=0, tiled=True)  14.5 us
    all_to_all x1, starting transfers between devices, per_device(): lax.all_to_all(packets, ('row', 'col'), split_axis=0, concat_axis=0, tile...  10.3 us
    pallas_call x1, Pallas kernels, columns(): pl.pallas_call(columns_kernel, grid=(colors,), in_specs=[smem, smem, bloc...  9.37 us
    pallas_call x1, Pallas kernels, rows_inverse(): pl.pallas_call(rows_inverse_kernel, grid=(colors,), in_specs=[pl.BlockSpe...  9.14 us
    ppermute x2, starting transfers between devices, extended(): before = lax.ppermute(last, axis, up)  8.66 us
  transfers between devices with their start and end apart: 5, of which 1 were waited for; matrix products, arithmetic and copies ran while one was open for 11% of the time, Pallas kernels for 0%

commit v1 on v0

--- a/solution.py
+++ b/solution.py
@@ -151,12 +151,85 @@
 NT = ((1,), (1,))
 
 
-def rows_forward_kernel(phase_ref, matrix_ref, twist_ref, out_ref, hi_ref, lo_ref):
+LOGICAL = pl.DeviceIdType.LOGICAL
+
+
+def enter(me, free, members):
+    barrier = pltpu.get_barrier_semaphore()
+    row, col = me // members, me % members
+    rows = 128 // members
+
+    def signal(sem, device):
+        pl.semaphore_signal(sem, inc=1, device_id=device, device_id_type=LOGICAL)
+
+    def up():
+        @pl.when(row > 0)
+        def _():
+            signal(barrier, col)
+
+    def down():
+        @pl.when(row > 0)
+        def _():
+            pl.semaphore_wait(free, 1)
+
+        @pl.when((row == 0) & (col > 0))
+        def _():
+            pl.semaphore_wait(barrier, rows - 1)
+            signal(barrier, 0)
+            pl.semaphore_wait(free, 1)
+
+        @pl.when(me == 0)
+        def _():
+            pl.semaphore_wait(barrier, rows - 1 + members - 1)
+
+            def tell(k, carry):
+                signal(free, k)
+                return carry
+
+            lax.fori_loop(1, members, tell, 0)
+
+        @pl.when(row == 0)
+        def _():
+            def tell(k, carry):
+                signal(free, k * members + col)
+                return carry
+
+            lax.fori_loop(1, rows, tell, 0)
+
+    return up, down
+
+
+def send_all(me, block_of, landing, send_sem, recv_sem, local_sem):
+    pltpu.make_async_copy(block_of(me), landing.at[me], local_sem).start()
+
+    def step(k, carry):
+        peer = (me + k) % 128
+        pltpu.make_async_remote_copy(
+            src_ref=block_of(peer),
+            dst_ref=landing.at[me],
+            send_sem=send_sem,
+            recv_sem=recv_sem,
+            device_id=peer,
+            device_id_type=LOGICAL,
+        ).start()
+        return carry
+
+    lax.fori_loop(1, 128, step, 0)
+
+
+def wait_all(landing, send_sem, recv_sem, local_sem):
+    pltpu.make_async_copy(landing.at[0], landing.at[0], local_sem).wait()
+    others = landing.at[pl.ds(0, 127)]
+    pltpu.make_async_copy(others, others, send_sem).wait()
+    pltpu.make_async_copy(others, others, recv_sem).wait()
+
+
+def rows_forward(o, phase_ref, matrix_ref, twist_ref, out_ref, hi_ref, lo_ref):
     for half in range(2):
         cols = pl.ds(half * 128, 128)
         field = []
         for j in range(16):
-            field.append(cos_sin_quarters(2.0 * decode(phase_ref[j, :, cols])))
+            field.append(cos_sin_quarters(2.0 * decode(phase_ref[j, o, :, cols])))
         spectrum = fft16(field, -1.0)
         for k1 in range(16):
             re, im = spectrum[k1]
@@ -172,24 +245,46 @@
                 lo_ref[rows, place] = lo
     result = dot3((matrix_ref[0], matrix_ref[1]), (hi_ref[...], lo_ref[...]), NT)
     for h in range(2):
-        out_ref[:, h] = encode(result[:, h * 128 : (h + 1) * 128]).reshape(64, 8, 128)
-
-
-def columns_kernel(wave_ref, travel_ref, in_ref, matrix_ref, back_ref, twist_ref, out_ref, re_ref, im_ref, hi_ref, lo_ref):
-    color = pl.program_id(0)
-    position = lax.axis_index("row") * 16 + lax.axis_index("col")
+        out_ref[:, h, o] = encode(result[:, h * 128 : (h + 1) * 128]).reshape(64, 8, 128)
+
+
+def transfer(o, me, wave, travel, cos_ref, sin_ref):
     row = lax.broadcasted_iota(jnp.int32, (8, 128), 0)
     lane = lax.broadcasted_iota(jnp.int32, (8, 128), 1)
+    base_x = (row // 4) + 128 * (lane % 16)
+    freq_y = 8 * (me % 2) + lane // 16 + 16 * (4 * (me // 2) + row % 4)
+    signed_y = jnp.where(freq_y < 2048, freq_y, freq_y - 4096).astype(F32) * (1.0 / 4096)
+    square_y = signed_y * signed_y
+
+    def step(place, carry):
+        freq_x = base_x + 2 * place
+        signed_x = jnp.where(freq_x < 1024, freq_x, freq_x - 2048).astype(F32) * (1.0 / 2048)
+        squared = signed_x * signed_x + square_y
+        turns = travel * squared / (wave + jnp.sqrt(wave * wave - squared))
+        c, w = cos_sin_quarters(4.0 * turns)
+        cos_ref[o, place] = c
+        sin_ref[o, place] = w
+        return carry
+
+    lax.fori_loop(0, 64, step, 0, unroll=4)
+
+
+def put_split(place, re, im, hi_ref, lo_ref):
+    for part, value in enumerate((re, im)):
+        hi, lo = split(value)
+        lanes = pl.ds(part * 128, 128)
+        hi_ref[place, :, lanes] = hi
+        lo_ref[place, :, lanes] = lo
+
+
+def columns(o, in_ref, matrix_ref, back_ref, twist_ref, cos_ref, sin_ref, out_ref, re_ref, im_ref, hi_ref, lo_ref):
+    row = lax.broadcasted_iota(jnp.int32, (8, 128), 0)
     top = row < 4
-
-    def tile(ref, k):
-        return ref[k, 0]
-
     for n2 in range(8):
         column = []
         for n1 in range(8):
             s = 8 * n1 + n2
-            a, b = decode(tile(in_ref, s)), decode(tile(in_ref, s + 64))
+            a, b = decode(in_ref[s, o]), decode(in_ref[s + 64, o])
             total, delta = a + b, a - b
             re = jnp.where(top, total, pltpu.roll(delta, 4, 0))
             im = jnp.where(top, pltpu.roll(total, 4, 0), delta)
@@ -205,40 +300,16 @@
             im_ref[m1 * 8 + n2] = im
     for m1 in range(8):
         column = [(re_ref[m1 * 8 + n2], im_ref[m1 * 8 + n2]) for n2 in range(8)]
-        points = fft8(column, -1.0)
-        for pair in range(0, 8, 1):
-            place = m1 + 8 * pair
-            re, im = points[pair]
+        for m2, (re, im) in enumerate(fft8(column, -1.0)):
+            place = m1 + 8 * m2
             c, w = twist_ref[0, place], twist_ref[1, place]
-            re, im = re * c - im * w, re * w + im * c
-            hi_re, lo_re = split(re)
-            hi_im, lo_im = split(im)
-            hi_ref[place, :, :128] = hi_re
-            hi_ref[place, :, 128:] = hi_im
-            lo_ref[place, :, :128] = lo_re
-            lo_ref[place, :, 128:] = lo_im
+            put_split(place, re * c - im * w, re * w + im * c, hi_ref, lo_ref)
     data = (hi_ref[...].reshape(512, 256), lo_ref[...].reshape(512, 256))
     spectrum = dot3(data, (matrix_ref[0], matrix_ref[1]), NN).reshape(64, 8, 256)
-    wave = wave_ref[color]
-    travel = travel_ref[0]
-    base_x = (row // 4) + 128 * (lane % 16)
-    freq_y = 8 * (position % 2) + lane // 16 + 16 * (4 * (position // 2) + row % 4)
-    signed_y = jnp.where(freq_y < 2048, freq_y, freq_y - 4096).astype(F32) * (1.0 / 4096)
-    square_y = signed_y * signed_y
     for place in range(64):
-        freq_x = base_x + 2 * place
-        signed_x = jnp.where(freq_x < 1024, freq_x, freq_x - 2048).astype(F32) * (1.0 / 2048)
-        squared = signed_x * signed_x + square_y
-        turns = travel * squared / (wave + jnp.sqrt(wave * wave - squared))
-        c, w = cos_sin_quarters(4.0 * turns)
+        c, w = cos_ref[o, place], sin_ref[o, place]
         re, im = spectrum[place, :, :128], spectrum[place, :, 128:]
-        re, im = re * c + im * w, im * c - re * w
-        hi_re, lo_re = split(re)
-        hi_im, lo_im = split(im)
-        hi_ref[place, :, :128] = hi_re
-        hi_ref[place, :, 128:] = hi_im
-        lo_ref[place, :, :128] = lo_re
-        lo_ref[place, :, 128:] = lo_im
+        put_split(place, re * c + im * w, im * c - re * w, hi_ref, lo_ref)
     data = (hi_ref[...].reshape(512, 256), lo_ref[...].reshape(512, 256))
     spectrum = dot3(data, (back_ref[0], back_ref[1]), NN).reshape(64, 8, 256)
     for m1 in range(8):
@@ -263,13 +334,13 @@
                 re, im = re * c - im * w, im * c + re * w
             total = jnp.where(top, re, pltpu.roll(im, 4, 0))
             delta = jnp.where(top, pltpu.roll(re, 4, 0), im)
-            out_ref[s, 0] = encode(total + delta)
-            out_ref[s + 64, 0] = encode(total - delta)
-
-
-def rows_inverse_kernel(in_ref, matrix_ref, twist_ref, spread_ref, out_ref):
-    left = decode(in_ref[:, 0]).reshape(512, 128)
-    right = decode(in_ref[:, 1]).reshape(512, 128)
+            out_ref[s, o] = encode(total + delta)
+            out_ref[s + 64, o] = encode(total - delta)
+
+
+def rows_inverse(o, in_ref, matrix_ref, twist_ref, spread_ref, out_ref):
+    left = decode(in_ref[:, 0, o]).reshape(512, 128)
+    right = decode(in_ref[:, 1, o]).reshape(512, 128)
     data = split(jnp.concatenate([left, right], axis=1))
     value = dot3((matrix_ref[0], matrix_ref[1]), data, NN)
     re, im = value[:256], value[256:]
@@ -279,66 +350,73 @@
     for part in range(2):
         for j in range(16):
             rows = result[part * 256 + j * 16 : part * 256 + j * 16 + 16, :]
-            out_ref[part, :, j * 256 : (j + 1) * 256] = rows.astype(BF16)
-
-
-def whole(array):
-    return pl.BlockSpec(array.shape, lambda o: (0,) * array.ndim, pipeline_mode=pl.Buffered(1))
-
-
-def params():
-    return pltpu.CompilerParams(dimension_semantics=("arbitrary",), vmem_limit_bytes=VMEM_LIMIT)
-
-
-def rows_forward(phase, table):
+            out_ref[o, part, :, j * 256 : (j + 1) * 256] = rows.astype(BF16)
+
+
+def spectral_kernel(
+    wave_ref, travel_ref, phase_ref, forward_ref, inverse_ref, spread_ref, lanes_ref, back_ref, twist_y_ref, twist_back_ref, twist_x_ref,
+    out_ref,
+    packets_ref, spread_in_ref, filtered_ref, returned_ref, cos_ref, sin_ref, re_ref, im_ref, hi_ref, lo_ref, field_hi_ref, field_lo_ref,
+    free_sem, send_sems, recv_sems, local_sems,
+):
+    colors = phase_ref.shape[1]
+    me = lax.axis_index("row") * 16 + lax.axis_index("col")
+    up, down = enter(me, free_sem, 16)
+    up()
+
+    def each(body):
+        def step(o, carry):
+            body(o)
+            return carry
+
+        lax.fori_loop(0, colors, step, 0)
+
+    by_pair = packets_ref.reshape(64, 2, colors, 8, 128)
+    each(lambda o: rows_forward(o, phase_ref, forward_ref, twist_y_ref, by_pair, field_hi_ref, field_lo_ref))
+    down()
+    first = (send_sems.at[0], recv_sems.at[0], local_sems.at[0])
+    second = (send_sems.at[1], recv_sems.at[1], local_sems.at[1])
+    send_all(me, lambda d: packets_ref.at[d], spread_in_ref, *first)
+    each(lambda o: transfer(o, me, wave_ref[o], travel_ref[0], cos_ref, sin_ref))
+    wait_all(spread_in_ref, *first)
+    each(lambda o: columns(o, spread_in_ref, lanes_ref, back_ref, twist_x_ref, cos_ref, sin_ref, filtered_ref, re_ref, im_ref, hi_ref, lo_ref))
+    send_all(me, lambda d: filtered_ref.at[d], returned_ref, *second)
+    wait_all(returned_ref, *second)
+    by_pair_back = returned_ref.reshape(64, 2, colors, 8, 128)
+    each(lambda o: rows_inverse(o, by_pair_back, inverse_ref, twist_back_ref, spread_ref, out_ref))
+
+
+def spectral(phase, wave, travel):
+    table = tables()
     colors = phase.shape[1]
-    args = (jnp.asarray(table["forward_y"]), jnp.asarray(table["twist_y"]))
+    names = ("forward_y", "inverse_y", "spread16", "lanes", "lanes_back", "twist_y", "twist_back", "twist_x")
+    args = [jnp.asarray(table[k]) for k in names]
+    smem = pl.BlockSpec(memory_space=pltpu.SMEM)
+    vmem = pl.BlockSpec(memory_space=pltpu.VMEM)
+    exchange = pltpu.VMEM((128, colors, 8, 128), BF16)
     return pl.pallas_call(
-        rows_forward_kernel,
-        grid=(colors,),
-        in_specs=[pl.BlockSpec((16, None, 16, 256), lambda o: (0, o, 0, 0)), whole(args[0]), whole(args[1])],
-        out_specs=pl.BlockSpec((64, 2, None, 8, 128), lambda o: (0, 0, o, 0, 0)),
-        out_shape=jax.ShapeDtypeStruct((64, 2, colors, 8, 128), BF16),
-        scratch_shapes=[pltpu.VMEM((256, 512), BF16), pltpu.VMEM((256, 512), BF16)],
-        compiler_params=params(),
-        name="rows_forward",
-    )(phase, *args)
-
-
-def columns(spread, wave, travel, table):
-    colors = spread.shape[1]
-    args = tuple(jnp.asarray(table[k]) for k in ("lanes", "lanes_back", "twist_x"))
-    block = pl.BlockSpec((128, 1, 8, 128), lambda o: (0, o, 0, 0))
-    smem = pl.BlockSpec(memory_space=pltpu.SMEM)
-    return pl.pallas_call(
-        columns_kernel,
-        grid=(colors,),
-        in_specs=[smem, smem, block] + [whole(a) for a in args],
-        out_specs=block,
-        out_shape=jax.ShapeDtypeStruct((128, colors, 8, 128), BF16),
+        spectral_kernel,
+        in_specs=[smem, smem] + [vmem] * (1 + len(args)),
+        out_specs=vmem,
+        out_shape=jax.ShapeDtypeStruct((colors, 2, 16, 4096), BF16),
         scratch_shapes=[
+            exchange, exchange, exchange, exchange,
+            pltpu.VMEM((colors, 64, 8, 128), F32),
+            pltpu.VMEM((colors, 64, 8, 128), F32),
             pltpu.VMEM((64, 8, 128), F32),
             pltpu.VMEM((64, 8, 128), F32),
             pltpu.VMEM((64, 8, 256), BF16),
             pltpu.VMEM((64, 8, 256), BF16),
+            pltpu.VMEM((256, 512), BF16),
+            pltpu.VMEM((256, 512), BF16),
+            pltpu.SemaphoreType.REGULAR,
+            pltpu.SemaphoreType.DMA((2,)),
+            pltpu.SemaphoreType.DMA((2,)),
+            pltpu.SemaphoreType.DMA((2,)),
         ],
-        compiler_params=params(),
-        name="columns",
-    )(wave, travel, spread, *args)
-
-
-def rows_inverse(returned, table):
-    colors = returned.shape[2]
-    args = tuple(jnp.asarray(table[k]) for k in ("inverse_y", "twist_back", "spread16"))
-    return pl.pallas_call(
-        rows_inverse_kernel,
-        grid=(colors,),
-        in_specs=[pl.BlockSpec((64, 2, None, 8, 128), lambda o: (0, 0, o, 0, 0))] + [whole(a) for a in args],
-        out_specs=pl.BlockSpec((None, 2, 16, 4096), lambda o: (o, 0, 0, 0)),
-        out_shape=jax.ShapeDtypeStruct((colors, 2, 16, 4096), BF16),
-        compiler_params=params(),
-        name="rows_inverse",
-    )(returned, *args)
+        compiler_params=pltpu.CompilerParams(collective_id=0, has_side_effects=True, vmem_limit_bytes=VMEM_LIMIT),
+        name="spectral",
+    )(wave, travel, phase, *args)
 
 
 def extended(x, sides, width):
@@ -369,18 +447,13 @@
 
 
 def per_device(features, conv_weight, bias, inv_wavelength, distance):
-    table = tables()
     tile_rows, tile_cols = features.shape[1:]
     padded = extended(features, (("row", 1), ("col", 2)), 1)
     score = head_conv(padded, conv_weight, tile_rows, tile_cols)
     coded = encode(jnp.tanh(score + bias[:, None, None]))
     coded = coded.reshape(3, 16, 16, 256).transpose(1, 0, 2, 3)
     pencils = lax.all_to_all(coded, "col", split_axis=0, concat_axis=0, tiled=True)
-    packets = rows_forward(pencils, table).reshape(128, 3, 8, 128)
-    spread = lax.all_to_all(packets, ("row", "col"), split_axis=0, concat_axis=0, tiled=True)
-    packets = columns(spread, inv_wavelength, distance, table)
-    returned = lax.all_to_all(packets, ("row", "col"), split_axis=0, concat_axis=0, tiled=True)
-    return rows_inverse(returned.reshape(64, 2, 3, 8, 128), table)
+    return spectral(pencils, inv_wavelength, distance)
 
 
 def solution(mesh):

time: 133 us -> 117 us (0.88)
  blocking collectives: 36.4 us -> 0 us
  Pallas kernels: 24.7 us -> 55.8 us
  waiting for transfers between devices: 16.2 us -> 7.63 us
  starting transfers between devices: 22.4 us -> 18.5 us
  local copies, waits for them, and re-layouts: 14.1 us -> 16.7 us
    all_to_all x2 -> x0, blocking collectives: 36.4 us -> none  [the longest x1 21.9 us: per_device(): lax.all_to_all(packets, ('row', 'col'), split_axis=0, concat_axis=0, tile...]
    pallas_call x3 -> x1, Pallas kernels: 24.7 us -> 55.8 us  [spectral(): pl.pallas_call(spectral_kernel, in_specs=[smem, smem] + [vmem] * (1 + len...]
    all_to_all x1, waiting for transfers between devices: 16.2 us -> 7.62 us  [per_device(): lax.all_to_all(coded, 'col', split_axis=0, concat_axis=0, tiled=True)]
    all_to_all x1, starting transfers between devices: 10.3 us -> 6.3 us  [per_device(): lax.all_to_all(coded, 'col', split_axis=0, concat_axis=0, tiled=True)]
    unnamed x27 -> x28, local copies, waits for them, and re-layouts: 6.07 us -> 8 us
  transfers between devices with their start and end apart: 5 -> 5, of which waited for: 1 -> 1; matrix products, arithmetic and copies ran while one was open for 11% -> 12% of each run, Pallas kernels for 0% -> 0%
where the time goes in v1:
time: 117 us
  Pallas kernels  55.8 us (48%)
  starting transfers between devices  18.5 us (16%)
  local copies, waits for them, and re-layouts  16.7 us (14%)
  matrix products  16.4 us (14%)
  waiting for transfers between devices  7.63 us (7%)
  other arithmetic  1.19 us (1%)
    pallas_call x1, Pallas kernels, spectral(): pl.pallas_call(spectral_kernel, in_specs=[smem, smem] + [vmem] * (1 + len...  55.8 us
    dot_general x9, matrix products, head_conv(): jnp.einsum('oc,cxy->oxy', conv_weight[:, :, shift_u, shift_v], window, pr...  16.4 us
    ppermute x2, starting transfers between devices, extended(): before = lax.ppermute(last, axis, up)  8.66 us
    unnamed x28, local copies, waits for them, and re-layouts  8 us
    all_to_all x1, waiting for transfers between devices, per_device(): lax.all_to_all(coded, 'col', split_axis=0, concat_axis=0, tiled=True)  7.62 us
    all_to_all x1, starting transfers between devices, per_device(): lax.all_to_all(coded, 'col', split_axis=0, concat_axis=0, tiled=True)  6.3 us
    slice x2, local copies, waits for them, and re-layouts, extended(): last = lax.slice_in_dim(x, length - width, length, axis=dim)  3.61 us
    ppermute x2, starting transfers between devices, extended(): after = lax.ppermute(first, axis, down)  3.52 us
  transfers between devices with their start and end apart: 5, of which 1 were waited for; matrix products, arithmetic and copies ran while one was open for 12% of the time, Pallas kernels for 0%

profile of v1, /device:TPU:1, one launch (start us, length us, event | category | flops | bytes accessed | tf_op | source)
XLA Modules:
  0.0 117.0 jit_solution(243493189087570164)
XLA Ops:
  0.0 0.0 copy-start
  0.0 0.0 copy-start.10
  0.0 2.9 %copy.40 = bf16[16,256,256]{2,0,1:T(8,128)(2,1)S(1)} copy(bf16[16,256,256]{2,1,0:T(8,128)(2,1)} %param.13) | data formatting | bytes 4194304 | tf_op args[0]
  2.9 0.0 copy-start.3
  3.0 4.0 %collective-permute-start = (bf16[16,1,256]{2,0,1:T(8,128)(2,1)S(1)}, bf16[16,1,256]{2,0,1:T(8,128)(2,1)S(1)}, u32[]{:S(2)}, u32[]{:S(2)}) collective-permute-start(bf16[16,1,256]{2,0,1:T(8,128)(2,1)S(1)} %get-tuple-element.8), channel_id=1, source_target_pairs={{0,16},{16,32},{32,48},{48,64},{64,80},{80,96},{96,112},{1,17},{17... | collective-permute-start | bytes 24584 | tf_op jit(solution)/shard_map/ppermute | solution.py:429
  7.0 1.3 %collective-permute-start.1 = (bf16[16,1,256]{2,0,1:T(8,128)(2,1)S(1)}, bf16[16,1,256]{2,0,1:T(8,128)(2,1)S(1)}, u32[]{:S(2)}, u32[]{:S(2)}) collective-permute-start(bf16[16,1,256]{2,0,1:T(8,128)(2,1)S(1)} %get-tuple-element.7), channel_id=1, source_target_pairs={{16,0},{32,16},{48,32},{64,48},{80,64},{96,80},{112,96},{17,1},{33... | collective-permute-start | bytes 24584 | tf_op jit(solution)/shard_map/ppermute | solution.py:430
  8.3 0.0 copy-done.10
  8.3 0.0 copy-done
  8.3 2.3 %fusion.35 = f32[3,256,256]{2,0,1:T(4,128)} fusion(bf16[3,16,1,1]{1,3,2,0:T(2,128)(2,1)S(1)} %get-tuple-element.12, bf16[16,256,256]{2,1,0:T(8,128)(2,1)S(1)} %copy-done), kind=kOutput, calls=%fused_computation.56 | convolution fusion | flops 6291456 | bytes 2883680 | tf_op jit(solution)/shard_map/oc,cxy->oxy/dot_general | solution.py:440
  10.6 0.0 collective-permute-done
  10.6 1.2 %constant_dynamic-update-slice_fusion.1 = bf16[16,258,256]{2,0,1:T(8,128)(2,1)S(1)} fusion(bf16[16,258,256]{2,0,1:T(8,128)(2,1)S(1)} %constant_dynamic-update-slice_fusion.2, bf16[16,256,256]{2,1,0:T(8,128)(2,1)S(1)} %copy-done), kind=kLoop, calls=%fused_computation.46 | loop fusion | bytes 4194304
  11.8 0.0 copy-done.3
  11.8 0.0 collective-permute-done.1
  11.9 1.5 %fusion.55 = (bf16[16,258,1]{2,0,1:T(8,128)(2,1)}, bf16[16,258,1]{2,0,1:T(8,128)(2,1)S(1)}) fusion(bf16[16,258,256]{2,0,1:T(8,128)(2,1)S(1)} %constant_dynamic-update-slice_fusion), kind=kLoop, calls=%fused_computation.76 | loop fusion | bytes 33024 | tf_op jit(solution)/shard_map/slice | solution.py:427
  13.3 2.1 %copy.43 = bf16[16,258,1]{1,0,2:T(8,128)(2,1)S(1)} copy(bf16[16,258,1]{2,0,1:T(8,128)(2,1)} %get-tuple-element.5) | data formatting | bytes 16512 | tf_op jit(solution)/shard_map/slice | solution.py:427
  15.5 4.6 %collective-permute-start.2 = (bf16[16,258,1]{1,0,2:T(8,128)(2,1)S(1)}, bf16[16,258,1]{1,0,2:T(8,128)(2,1)S(1)}, u32[]{:S(2)}, u32[]{:S(2)}) collective-permute-start(bf16[16,258,1]{1,0,2:T(8,128)(2,1)S(1)} %copy.43), channel_id=1, source_target_pairs={{0,1},{1,2},{2,3},{3,4},{4,5},{5,6},{6,7},{7,8},{8,9},{9,10},{10,1... | collective-permute-start | bytes 24776 | tf_op jit(solution)/shard_map/ppermute | solution.py:429
  20.1 1.1 copy.48
  21.2 0.0 copy-start.4
  21.2 2.2 %collective-permute-start.3 = (bf16[16,258,1]{1,0,2:T(8,128)(2,1)S(1)}, bf16[16,258,1]{1,0,2:T(8,128)(2,1)S(1)}, u32[]{:S(2)}, u32[]{:S(2)}) collective-permute-start(bf16[16,258,1]{1,0,2:T(8,128)(2,1)S(1)} %copy.48), channel_id=1, source_target_pairs={{1,0},{2,1},{3,2},{4,3},{5,4},{6,5},{7,6},{8,7},{9,8},{10,9},{11,1... | collective-permute-start | bytes 24776 | tf_op jit(solution)/shard_map/ppermute | solution.py:430
  23.4 3.0 %fusion = f32[256,256,3]{1,2,0:T(4,128)} fusion(bf16[16,256,256]{2,0,1:T(8,128)(2,1)} %copy-done.3, bf16[16,1,256]{2,0,1:T(8,128)(2,1)S(1)} %collective-permute-done, bf16[3,16,1,1]{1,3,2,0:T(2,128)(2,1)S(1)} %get-tuple-element.15), kind=kOutput, calls=%fused_computation.8 | convolution fusion | flops 10502144 | bytes 2891872 | tf_op jit(solution)/shard_map/oc,cxy->oxy/dot_general | solution.py:440
  26.4 0.0 copy-done.4
  26.4 1.4 %fusion.4 = f32[256,256,3]{1,2,0:T(4,128)} fusion(bf16[16,1,256]{2,0,1:T(8,128)(2,1)S(1)} %collective-permute-done.1, bf16[16,256,256]{2,0,1:T(8,128)(2,1)S(1)} %copy-done.4, bf16[3,16,1,1]{1,3,2,0:T(2,128)(2,1)S(1)} %get-tuple-element.17), kind=kOutput, calls=%fused_computation.12 | convolution fusion | flops 10502144 | bytes 2891872 | tf_op jit(solution)/shard_map/oc,cxy->oxy/dot_general | solution.py:440
  27.8 0.0 collective-permute-done.2
  27.8 1.2 %copy.44 = bf16[16,258,1]{2,0,1:T(8,128)(2,1)S(1)} copy(bf16[16,258,1]{1,0,2:T(8,128)(2,1)S(1)} %collective-permute-done.2) | data formatting | bytes 16512 | tf_op jit(solution)/shard_map/ppermute | solution.py:429
  29.0 2.0 %fusion.16 = f32[256,256,3]{1,2,0:T(4,128)} fusion(bf16[16,258,256]{2,0,1:T(8,128)(2,1)S(1)} %constant_dynamic-update-slice_fusion, bf16[16,258,1]{2,0,1:T(8,128)(2,1)S(1)} %copy.44, bf16[3,16,1,1]{1,3,2,0:T(2,128)(2,1)S(1)} %get-tuple-element.9), kind=kOutput, calls=%fused_computation.26 | convolution fusion | flops 10485760 | bytes 2908320 | tf_op jit(solution)/shard_map/oc,cxy->oxy/dot_general | solution.py:440
  31.0 2.0 %fusion.18 = f32[256,256,3]{1,2,0:T(4,128)} fusion(bf16[16,258,256]{2,0,1:T(8,128)(2,1)S(1)} %constant_dynamic-update-slice_fusion, bf16[16,258,1]{2,0,1:T(8,128)(2,1)S(1)} %copy.44, bf16[3,16,1,1]{1,3,2,0:T(2,128)(2,1)S(1)} %get-tuple-element.13), kind=kOutput, calls=%fused_computation.27 | convolution fusion | flops 10485760 | bytes 2908320 | tf_op jit(solution)/shard_map/oc,cxy->oxy/dot_general | solution.py:440
  32.9 0.0 collective-permute-done.3
  32.9 2.1 %copy.49 = bf16[16,258,1]{2,0,1:T(8,128)(2,1)} copy(bf16[16,258,1]{1,0,2:T(8,128)(2,1)S(1)} %collective-permute-done.3) | data formatting | bytes 16512 | tf_op jit(solution)/shard_map/ppermute | solution.py:430
  35.0 0.0 copy-start.1
  35.0 2.5 %fusion.20 = f32[256,256,3]{1,2,0:T(4,128)S(1)} fusion(bf16[16,258,256]{2,0,1:T(8,128)(2,1)S(1)} %constant_dynamic-update-slice_fusion, bf16[16,258,1]{2,0,1:T(8,128)(2,1)} %copy.49, bf16[3,16,1,1]{1,3,2,0:T(2,128)(2,1)S(1)} %get-tuple-element.14), kind=kOutput, calls=%fused_computation.28 | convolution fusion | flops 10485760 | bytes 2908320 | tf_op jit(solution)/shard_map/oc,cxy->oxy/dot_general | solution.py:440
  37.5 0.0 copy-done.1
  37.5 1.2 fusion.22
  38.7 0.0 copy-start.9
  38.7 1.0 fusion.14
  39.6 0.0 copy-start.2
  39.7 0.0 copy-start.6
  39.7 0.0 copy-start.7
  39.7 0.0 copy-start.8
  39.7 0.0 copy-start.11
  39.7 1.1 fusion.12
  40.8 0.0 copy-done.9
  40.8 0.1 copy-done.2
  40.9 0.3 copy-done.6
  41.3 0.3 copy-done.7
  41.6 0.3 copy-done.8
  41.9 0.0 copy-done.11
  41.9 1.2 %fusion.24 = bf16[3,256,256]{2,1,0:T(8,128)(2,1)S(1)} fusion(f32[256,256,3]{1,2,0:T(4,128)S(1)} %fusion.12, f32[256,256,3]{1,2,0:T(4,128)S(1)} %copy-done.7, f32[256,256,3]{1,2,0:T(4,128)S(1)} %fusion.14, f32[256,256,3]{1,2,0:T(4,128)S(1)} %fusion.22, f32[3,256,256]{2,0,1:T(4,128)S(1)} %copy-done.2, f32[256,256,3]{1,2,0:T(4,128)S(1)} %copy-done.9, ...), kind=kLoop, calls=%fused_computation.33 | loop fusion | flops 3145728 | bytes 7471116 | tf_op jit(solution)/shard_map/convert_element_type | solution.py:66
  43.1 0.8 copy.124
  43.8 6.3 %all-to-all-start = ((bf16[16,3,16,256]{3,2,1,0:T(8,128)(2,1)}), bf16[16,3,16,256]{3,2,1,0:T(8,128)(2,1)S(1)}, u32[]{:S(2)}, u32[]{:S(2)}) async-start(bf16[16,3,16,256]{3,2,1,0:T(8,128)(2,1)} %bitcast.54), calls=%async_computation | async-start | bytes 786432 | tf_op jit(solution)/shard_map/all_to_all | solution.py:455
  50.8 7.6 %all-to-all-done.phase_ref = bf16[16,3,16,256]{3,2,1,0:T(8,128)(2,1)S(1)} async-done(((bf16[16,3,16,256]{3,2,1,0:T(8,128)(2,1)}), bf16[16,3,16,256]{3,2,1,0:T(8,128)(2,1)S(1)}, u32[]{:S(2)}, u32[]{:S(2)}) %all-to-all-start) | async-done | bytes 393248 | tf_op jit(solution)/shard_map/all_to_all | solution.py:455
  58.4 0.0 copy-start.5
  58.4 0.7 copy-done.5
  59.2 55.8 %spectral.1 = bf16[3,2,16,4096]{3,2,1,0:T(8,128)(2,1)} custom-call(f32[3]{0:T(128)} %wave_ref.1, f32[1]{0:T(128)S(6)} %copy.128.travel_ref, bf16[16,3,16,256]{3,2,1,0:T(8,128)(2,1)} %copy-done.5, bf16[2,512,512]{2,1,0:T(8,128)(2,1)} %constant.16.clone.forward_ref, bf16[2,512,512]{2,1,0:T(8,128)(2,1)} %constant.17.clone.inverse_ref, ...), custom_call_target="tpu_custom_call" | custom-call | tf_op jit(solution)/shard_map/spectral/pallas_call | solution.py:397
  114.9 2.1 %copy.129 = bf16[3,2,16,4096]{3,2,1,0:T(8,128)(2,1)} copy(bf16[3,2,16,4096]{3,2,1,0:T(8,128)(2,1)} %spectral.1) | data formatting | bytes 1572864
  (4 shorter events, 0.0 us)
Async XLA Ops:
  0.0 8.3 %copy-start = (bf16[16,256,256]{2,1,0:T(8,128)(2,1)S(1)}, bf16[16,256,256]{2,1,0:T(8,128)(2,1)}, u32[]{:S(2)}) copy-start(bf16[16,256,256]{2,1,0:T(8,128)(2,1)} %param.13) | copy-start | bytes 6291460
  0.0 8.3 %copy-start.10 = (bf16[3,16,3,3]{1,3,2,0:T(4,128)(2,1)S(1)}, bf16[3,16,3,3]{1,3,2,0:T(4,128)(2,1)}, u32[]{:S(2)}) copy-start(bf16[3,16,3,3]{1,3,2,0:T(4,128)(2,1)} %param.14) | copy-start | bytes 2596
  2.9 8.9 %copy-start.3 = (bf16[16,256,256]{2,0,1:T(8,128)(2,1)}, bf16[16,256,256]{2,0,1:T(8,128)(2,1)S(1)}, u32[]{:S(2)}) copy-start(bf16[16,256,256]{2,0,1:T(8,128)(2,1)S(1)} %copy.40) | copy-start | bytes 6291460
  3.0 7.7 %collective-permute-start = (bf16[16,1,256]{2,0,1:T(8,128)(2,1)S(1)}, bf16[16,1,256]{2,0,1:T(8,128)(2,1)S(1)}, u32[]{:S(2)}, u32[]{:S(2)}) collective-permute-start(bf16[16,1,256]{2,0,1:T(8,128)(2,1)S(1)} %get-tuple-element.8), channel_id=1, source_target_pairs={{0,16},{16,32},{32,48},{48,64},{64,80},{80,96},{96,112},{1,17},{17... | collective-permute-start | bytes 24584 | tf_op jit(solution)/shard_map/ppermute | solution.py:429
  7.0 4.8 %collective-permute-start.1 = (bf16[16,1,256]{2,0,1:T(8,128)(2,1)S(1)}, bf16[16,1,256]{2,0,1:T(8,128)(2,1)S(1)}, u32[]{:S(2)}, u32[]{:S(2)}) collective-permute-start(bf16[16,1,256]{2,0,1:T(8,128)(2,1)S(1)} %get-tuple-element.7), channel_id=1, source_target_pairs={{16,0},{32,16},{48,32},{64,48},{80,64},{96,80},{112,96},{17,1},{33... | collective-permute-start | bytes 24584 | tf_op jit(solution)/shard_map/ppermute | solution.py:430
  15.5 12.3 %collective-permute-start.2 = (bf16[16,258,1]{1,0,2:T(8,128)(2,1)S(1)}, bf16[16,258,1]{1,0,2:T(8,128)(2,1)S(1)}, u32[]{:S(2)}, u32[]{:S(2)}) collective-permute-start(bf16[16,258,1]{1,0,2:T(8,128)(2,1)S(1)} %copy.43), channel_id=1, source_target_pairs={{0,1},{1,2},{2,3},{3,4},{4,5},{5,6},{6,7},{7,8},{8,9},{9,10},{10,1... | collective-permute-start | bytes 24776 | tf_op jit(solution)/shard_map/ppermute | solution.py:429
  21.2 5.2 %copy-start.4 = (bf16[16,256,256]{2,0,1:T(8,128)(2,1)S(1)}, bf16[16,256,256]{2,0,1:T(8,128)(2,1)}, u32[]{:S(2)}) copy-start(bf16[16,256,256]{2,0,1:T(8,128)(2,1)} %copy-done.3) | copy-start | bytes 6291460
  21.2 11.7 %collective-permute-start.3 = (bf16[16,258,1]{1,0,2:T(8,128)(2,1)S(1)}, bf16[16,258,1]{1,0,2:T(8,128)(2,1)S(1)}, u32[]{:S(2)}, u32[]{:S(2)}) collective-permute-start(bf16[16,258,1]{1,0,2:T(8,128)(2,1)S(1)} %copy.48), channel_id=1, source_target_pairs={{1,0},{2,1},{3,2},{4,3},{5,4},{6,5},{7,6},{8,7},{9,8},{10,9},{11,1... | collective-permute-start | bytes 24776 | tf_op jit(solution)/shard_map/ppermute | solution.py:430
  35.0 2.5 %copy-start.1 = (bf16[16,258,1]{2,0,1:T(8,128)(2,1)S(1)}, bf16[16,258,1]{2,0,1:T(8,128)(2,1)}, u32[]{:S(2)}) copy-start(bf16[16,258,1]{2,0,1:T(8,128)(2,1)} %copy.49) | copy-start | bytes 24772
  38.7 2.2 %copy-start.9 = (f32[256,256,3]{1,2,0:T(4,128)S(1)}, f32[256,256,3]{1,2,0:T(4,128)}, u32[]{:S(2)}) copy-start(f32[256,256,3]{1,2,0:T(4,128)} %fusion.18) | copy-start | bytes 2359300
  39.6 1.3 %copy-start.2 = (f32[3,256,256]{2,0,1:T(4,128)S(1)}, f32[3,256,256]{2,0,1:T(4,128)}, u32[]{:S(2)}) copy-start(f32[3,256,256]{2,0,1:T(4,128)} %fusion.35) | copy-start | bytes 2359300
  39.7 1.6 %copy-start.6 = (f32[256,256,3]{1,2,0:T(4,128)S(1)}, f32[256,256,3]{1,2,0:T(4,128)}, u32[]{:S(2)}) copy-start(f32[256,256,3]{1,2,0:T(4,128)} %fusion) | copy-start | bytes 2359300
  39.7 1.9 %copy-start.7 = (f32[256,256,3]{1,2,0:T(4,128)S(1)}, f32[256,256,3]{1,2,0:T(4,128)}, u32[]{:S(2)}) copy-start(f32[256,256,3]{1,2,0:T(4,128)} %fusion.4) | copy-start | bytes 2359300
  39.7 2.2 %copy-start.8 = (f32[256,256,3]{1,2,0:T(4,128)S(1)}, f32[256,256,3]{1,2,0:T(4,128)}, u32[]{:S(2)}) copy-start(f32[256,256,3]{1,2,0:T(4,128)} %fusion.16) | copy-start | bytes 2359300
  39.7 2.2 %copy-start.11 = (f32[3]{0:T(128)S(1)}, f32[3]{0:T(128)}, u32[]{:S(2)}) copy-start(f32[3]{0:T(128)} %param.15) | copy-start | bytes 40
  43.8 14.6 %all-to-all-start = ((bf16[16,3,16,256]{3,2,1,0:T(8,128)(2,1)}), bf16[16,3,16,256]{3,2,1,0:T(8,128)(2,1)S(1)}, u32[]{:S(2)}, u32[]{:S(2)}) async-start(bf16[16,3,16,256]{3,2,1,0:T(8,128)(2,1)} %bitcast.54), calls=%async_computation | async-start | bytes 786432 | tf_op jit(solution)/shard_map/all_to_all | solution.py:455
  58.4 0.7 copy-start.5

commit v2 on v1

--- a/solution.py
+++ b/solution.py
@@ -219,7 +219,7 @@
 
 def wait_all(landing, send_sem, recv_sem, local_sem):
     pltpu.make_async_copy(landing.at[0], landing.at[0], local_sem).wait()
-    others = landing.at[pl.ds(0, 127)]
+    others = landing.at[pl.ds(0, landing.shape[0] - 1)]
     pltpu.make_async_copy(others, others, send_sem).wait()
     pltpu.make_async_copy(others, others, recv_sem).wait()
 
@@ -353,16 +353,151 @@
             out_ref[o, part, :, j * 256 : (j + 1) * 256] = rows.astype(BF16)
 
 
+def band(weight_ref, band_ref):
+    x = lax.broadcasted_iota(jnp.int32, (32, 128), 0)
+    lane = lax.broadcasted_iota(jnp.int32, (32, 128), 1)
+    shift = lane % 64 - x - 15
+    upper = lane < 64
+
+    def block(vo, carry):
+        for pair in range(8):
+            value = jnp.zeros((32, 128), F32)
+            for u in range(3):
+                base = (vo * 16 + 2 * pair) * 3 + u
+                both = jnp.where(upper, weight_ref[base], weight_ref[base + 3])
+                value = jnp.where(shift == u, both, value)
+            band_ref[pl.ds(pl.multiple_of(vo * 32, 32), 32), pair * 128 : (pair + 1) * 128] = value.astype(BF16)
+        return carry
+
+    lax.fori_loop(0, 9, block, 0)
+    row = lax.broadcasted_iota(jnp.int32, (16, 128), 0)
+    lane = lax.broadcasted_iota(jnp.int32, (16, 128), 1)
+    upper = lane < 64
+    for place, (source, u) in enumerate(((16, 2), (47, 0))):
+        here = lane % 64 == source
+        for pair in range(8):
+            value = jnp.zeros((16, 128), F32)
+            for vo in range(9):
+                base = (vo * 16 + 2 * pair) * 3 + u
+                both = jnp.where(upper, weight_ref[base], weight_ref[base + 3])
+                value = jnp.where(here & (row == vo), both, value)
+            band_ref[288 + 16 * place : 304 + 16 * place, pair * 128 : (pair + 1) * 128] = value.astype(BF16)
+
+
+def head(i, j, weight_ref, bias_ref, band_ref, tile_ref, sums_ref, sides_ref, edges_ref, got_sides_ref, got_edges_ref, phase_ref, down, border_sems, send_phase):
+    band(weight_ref, band_ref)
+    lane = lax.broadcasted_iota(jnp.int32, (32, 128), 1)
+    to_right = jnp.zeros((32, 128), F32)
+    to_left = jnp.zeros((32, 128), F32)
+    for k in range(8):
+        window = tile_ref[:, k * 32 : k * 32 + 64, :].reshape(1024, 256)
+        count = 320 if k in (0, 7) else 288
+        value = jnp.dot(band_ref[:count], window, preferred_element_type=F32)
+        sums_ref[k] = value[:288].reshape(9, 32, 256)
+        if k == 0:
+            edges_ref[0] = value[288:304]
+        if k == 7:
+            edges_ref[1] = value[304:320]
+        for o in range(3):
+            to_right = jnp.where(lane == 3 * k + o, value[o * 32 : o * 32 + 32, 255:256], to_right)
+            to_left = jnp.where(lane == 3 * k + o, value[192 + o * 32 : 224 + o * 32, 0:1], to_left)
+    sides_ref[0] = to_right
+    sides_ref[1] = to_left
+    down()
+    send_sems, recv_sems = border_sems
+    copies = []
+    for slot, step in enumerate((1, -1)):
+        copies.append((sides_ref.at[slot], got_sides_ref.at[slot], i, (j + step + 16) % 16))
+    for edge, down_step in enumerate((-1, 1)):
+        for side, step in enumerate((-1, 0, 1)):
+            copies.append((edges_ref.at[edge], got_edges_ref.at[edge * 3 + 2 - side], (i + down_step + 8) % 8, (j + step + 16) % 16))
+    copies = [
+        pltpu.make_async_remote_copy(
+            src_ref=source, dst_ref=target, send_sem=send_sems.at[n], recv_sem=recv_sems.at[n],
+            device_id=row * 16 + col, device_id_type=LOGICAL,
+        )
+        for n, (source, target, row, col) in enumerate(copies)
+    ]
+    for copy in copies:
+        copy.start()
+    for copy in copies:
+        copy.wait()
+    below, above = i < 7, i > 0
+    left, right = j > 0, j < 15
+    wide = lax.broadcasted_iota(jnp.int32, (32, 256), 1)
+    tall = lax.broadcasted_iota(jnp.int32, (32, 1), 0)
+
+    def rows_beyond(k, vo):
+        first = (tall == 0) & (k == 0) & above
+        last = (tall == 31) & (k == 7) & below
+        top = got_edges_ref[4, vo : vo + 1, :]
+        bottom = got_edges_ref[1, vo : vo + 1, :]
+        return jnp.where(first, top, jnp.where(last, bottom, 0.0))
+
+    def column_beyond(k, o, side):
+        sides = got_sides_ref[side]
+        value = jnp.sum(jnp.where(lane == 3 * k + o, sides, 0.0), axis=1, keepdims=True)
+        first = (tall == 0) & (k == 0) & above
+        last = (tall == 31) & (k == 7) & below
+        vo, y = (o, 255) if side == 0 else (6 + o, 0)
+        top = got_edges_ref[3 + 2 * side, vo : vo + 1, y : y + 1]
+        bottom = got_edges_ref[2 * side, vo : vo + 1, y : y + 1]
+        value = value + jnp.where(first, top, jnp.where(last, bottom, 0.0))
+        return jnp.where(left if side == 0 else right, value, 0.0)
+
+    def block(step, carry):
+        k = (j // 2 + step) % 8
+        for o in range(3):
+            first = sums_ref[k, o] + rows_beyond(k, o)
+            middle = sums_ref[k, 3 + o] + rows_beyond(k, 3 + o)
+            last = sums_ref[k, 6 + o] + rows_beyond(k, 6 + o)
+            first = jnp.where(wide == 0, column_beyond(k, o, 0), pltpu.roll(first, 1, 1))
+            last = jnp.where(wide == 255, column_beyond(k, o, 1), pltpu.roll(last, 255, 1))
+            value = encode(jnp.tanh(first + middle + last + bias_ref[o]))
+            phase_ref[2 * k, o] = value[:16]
+            phase_ref[2 * k + 1, o] = value[16:]
+        send_phase(2 * k)
+        send_phase(2 * k + 1)
+        return carry
+
+    lax.fori_loop(0, 8, block, 0)
+
+
 def spectral_kernel(
-    wave_ref, travel_ref, phase_ref, forward_ref, inverse_ref, spread_ref, lanes_ref, back_ref, twist_y_ref, twist_back_ref, twist_x_ref,
+    weight_ref, bias_ref, wave_ref, travel_ref, features_ref,
+    forward_ref, inverse_ref, spread_ref, lanes_ref, back_ref, twist_y_ref, twist_back_ref, twist_x_ref,
     out_ref,
+    tile_ref, band_ref, sums_ref, sides_ref, edges_ref, got_sides_ref, got_edges_ref, phase_ref, got_phase_ref,
     packets_ref, spread_in_ref, filtered_ref, returned_ref, cos_ref, sin_ref, re_ref, im_ref, hi_ref, lo_ref, field_hi_ref, field_lo_ref,
-    free_sem, send_sems, recv_sems, local_sems,
+    free_sem, tile_sem, border_send, border_recv, send_sems, recv_sems, local_sems,
 ):
-    colors = phase_ref.shape[1]
-    me = lax.axis_index("row") * 16 + lax.axis_index("col")
+    colors = 3
+    i, j = lax.axis_index("row"), lax.axis_index("col")
+    me = i * 16 + j
     up, down = enter(me, free_sem, 16)
     up()
+    load = pltpu.make_async_copy(features_ref, tile_ref.at[:, pl.ds(16, 256), :], tile_sem)
+    load.start()
+    tile_ref[:, 0:16, :] = jnp.zeros((16, 16, 256), BF16)
+    tile_ref[:, 272:288, :] = jnp.zeros((16, 16, 256), BF16)
+    load.wait()
+
+    def send_phase(peer):
+        @pl.when(peer == j)
+        def _():
+            pltpu.make_async_copy(phase_ref.at[peer], got_phase_ref.at[j], local_sems.at[2]).start()
+
+        @pl.when(peer != j)
+        def _():
+            pltpu.make_async_remote_copy(
+                src_ref=phase_ref.at[peer], dst_ref=got_phase_ref.at[j], send_sem=send_sems.at[2], recv_sem=recv_sems.at[2],
+                device_id=i * 16 + peer, device_id_type=LOGICAL,
+            ).start()
+
+    head(
+        i, j, weight_ref, bias_ref, band_ref, tile_ref, sums_ref, sides_ref, edges_ref, got_sides_ref, got_edges_ref, phase_ref,
+        down, (border_send, border_recv), send_phase,
+    )
 
     def each(body):
         def step(o, carry):
@@ -371,13 +506,13 @@
 
         lax.fori_loop(0, colors, step, 0)
 
-    by_pair = packets_ref.reshape(64, 2, colors, 8, 128)
-    each(lambda o: rows_forward(o, phase_ref, forward_ref, twist_y_ref, by_pair, field_hi_ref, field_lo_ref))
-    down()
     first = (send_sems.at[0], recv_sems.at[0], local_sems.at[0])
     second = (send_sems.at[1], recv_sems.at[1], local_sems.at[1])
+    each(lambda o: transfer(o, me, wave_ref[o], travel_ref[0], cos_ref, sin_ref))
+    wait_all(got_phase_ref, send_sems.at[2], recv_sems.at[2], local_sems.at[2])
+    by_pair = packets_ref.reshape(64, 2, colors, 8, 128)
+    each(lambda o: rows_forward(o, got_phase_ref, forward_ref, twist_y_ref, by_pair, field_hi_ref, field_lo_ref))
     send_all(me, lambda d: packets_ref.at[d], spread_in_ref, *first)
-    each(lambda o: transfer(o, me, wave_ref[o], travel_ref[0], cos_ref, sin_ref))
     wait_all(spread_in_ref, *first)
     each(lambda o: columns(o, spread_in_ref, lanes_ref, back_ref, twist_x_ref, cos_ref, sin_ref, filtered_ref, re_ref, im_ref, hi_ref, lo_ref))
     send_all(me, lambda d: filtered_ref.at[d], returned_ref, *second)
@@ -386,20 +521,30 @@
     each(lambda o: rows_inverse(o, by_pair_back, inverse_ref, twist_back_ref, spread_ref, out_ref))
 
 
-def spectral(phase, wave, travel):
+def per_device(features, conv_weight, bias, wave, travel):
     table = tables()
-    colors = phase.shape[1]
+    colors = 3
     names = ("forward_y", "inverse_y", "spread16", "lanes", "lanes_back", "twist_y", "twist_back", "twist_x")
     args = [jnp.asarray(table[k]) for k in names]
+    weight = conv_weight.astype(F32).transpose(3, 0, 1, 2).reshape(-1)
     smem = pl.BlockSpec(memory_space=pltpu.SMEM)
     vmem = pl.BlockSpec(memory_space=pltpu.VMEM)
     exchange = pltpu.VMEM((128, colors, 8, 128), BF16)
     return pl.pallas_call(
         spectral_kernel,
-        in_specs=[smem, smem] + [vmem] * (1 + len(args)),
+        in_specs=[smem] * 4 + [pl.BlockSpec(memory_space=pl.ANY)] + [vmem] * len(args),
         out_specs=vmem,
         out_shape=jax.ShapeDtypeStruct((colors, 2, 16, 4096), BF16),
         scratch_shapes=[
+            pltpu.VMEM((16, 288, 256), BF16),
+            pltpu.VMEM((320, 1024), BF16),
+            pltpu.VMEM((8, 9, 32, 256), F32),
+            pltpu.VMEM((2, 32, 128), F32),
+            pltpu.VMEM((2, 16, 256), F32),
+            pltpu.VMEM((2, 32, 128), F32),
+            pltpu.VMEM((6, 16, 256), F32),
+            pltpu.VMEM((16, colors, 16, 256), BF16),
+            pltpu.VMEM((16, colors, 16, 256), BF16),
             exchange, exchange, exchange, exchange,
             pltpu.VMEM((colors, 64, 8, 128), F32),
             pltpu.VMEM((colors, 64, 8, 128), F32),
@@ -410,50 +555,16 @@
             pltpu.VMEM((256, 512), BF16),
             pltpu.VMEM((256, 512), BF16),
             pltpu.SemaphoreType.REGULAR,
-            pltpu.SemaphoreType.DMA((2,)),
-            pltpu.SemaphoreType.DMA((2,)),
-            pltpu.SemaphoreType.DMA((2,)),
+            pltpu.SemaphoreType.DMA,
+            pltpu.SemaphoreType.DMA((8,)),
+            pltpu.SemaphoreType.DMA((8,)),
+            pltpu.SemaphoreType.DMA((3,)),
+            pltpu.SemaphoreType.DMA((3,)),
+            pltpu.SemaphoreType.DMA((3,)),
         ],
         compiler_params=pltpu.CompilerParams(collective_id=0, has_side_effects=True, vmem_limit_bytes=VMEM_LIMIT),
         name="spectral",
-    )(wave, travel, phase, *args)
-
-
-def extended(x, sides, width):
-    for axis, dim in sides:
-        peers, length = (lax.axis_size(axis), x.shape[dim])
-        up = [(i, (i + 1) % peers) for i in range(peers - 1)]
-        down = [(j, i) for i, j in up]
-        last = lax.slice_in_dim(x, length - width, length, axis=dim)
-        first = lax.slice_in_dim(x, 0, width, axis=dim)
-        before = lax.ppermute(last, axis, up)
-        after = lax.ppermute(first, axis, down)
-        x = jnp.concatenate([before, x, after], axis=dim)
-    return x
-
-
-def head_conv(padded, conv_weight, tile_rows, tile_cols):
-    score = jnp.zeros((conv_weight.shape[0], tile_rows, tile_cols), jnp.float32)
-    for shift_u in range(3):
-        for shift_v in range(3):
-            window = padded[:, shift_u : shift_u + tile_rows, shift_v : shift_v + tile_cols]
-            score = score + jnp.einsum(
-                "oc,cxy->oxy",
-                conv_weight[:, :, shift_u, shift_v],
-                window,
-                preferred_element_type=jnp.float32,
-            )
-    return score
-
-
-def per_device(features, conv_weight, bias, inv_wavelength, distance):
-    tile_rows, tile_cols = features.shape[1:]
-    padded = extended(features, (("row", 1), ("col", 2)), 1)
-    score = head_conv(padded, conv_weight, tile_rows, tile_cols)
-    coded = encode(jnp.tanh(score + bias[:, None, None]))
-    coded = coded.reshape(3, 16, 16, 256).transpose(1, 0, 2, 3)
-    pencils = lax.all_to_all(coded, "col", split_axis=0, concat_axis=0, tiled=True)
-    return spectral(pencils, inv_wavelength, distance)
+    )(weight, bias, wave, travel, features, *args)
 
 
 def solution(mesh):

time: 117 us -> 78.2 us (0.67)
  starting transfers between devices: 18.5 us -> 0 us
  Pallas kernels: 55.8 us -> 73.4 us
  matrix products: 16.4 us -> 0 us
  local copies, waits for them, and re-layouts: 16.7 us -> 2.98 us
  waiting for transfers between devices: 7.63 us -> 0 us
    pallas_call x1, Pallas kernels: 55.8 us -> 73.4 us  [per_device(): pl.pallas_call(spectral_kernel, in_specs=[smem] * 4 + [pl.BlockSpec(memor...]
    dot_general x9 -> x0, matrix products: 16.4 us -> none  [head_conv(): jnp.einsum('oc,cxy->oxy', conv_weight[:, :, shift_u, shift_v], window, pr...]
    ppermute x4 -> x0, starting transfers between devices: 12.2 us -> none  [the longest x2 8.66 us: extended(): before = lax.ppermute(last, axis, up)]
    all_to_all x1 -> x0, waiting for transfers between devices: 7.62 us -> none  [per_device(): lax.all_to_all(coded, 'col', split_axis=0, concat_axis=0, tiled=True)]
    all_to_all x1 -> x0, starting transfers between devices: 6.3 us -> none  [per_device(): lax.all_to_all(coded, 'col', split_axis=0, concat_axis=0, tiled=True)]
    unnamed x28 -> x1, local copies, waits for them, and re-layouts: 8 us -> 2.06 us
    slice x5 -> x0, local copies, waits for them, and re-layouts: 4.69 us -> none  [the longest x2 3.61 us: extended(): last = lax.slice_in_dim(x, length - width, length, axis=dim)]
    ppermute x2 -> x0, local copies, waits for them, and re-layouts: 3.28 us -> none  [the longest x1 2.11 us: extended(): after = lax.ppermute(first, axis, down)]
  transfers between devices with their start and end apart: 5 -> 0, of which waited for: 1 -> 0; matrix products, arithmetic and copies ran while one was open for 12% -> 0% of each run, Pallas kernels for 0% -> 0%
where the time goes in v2:
time: 78.2 us; the launch traced here: 77.8 us
  Pallas kernels  73.4 us (94%)
  local copies, waits for them, and re-layouts  2.98 us (4%)
    pallas_call x1, Pallas kernels, per_device(): pl.pallas_call(spectral_kernel, in_specs=[smem] * 4 + [pl.BlockSpec(memor...  73.4 us
    unnamed x1, local copies, waits for them, and re-layouts  2.06 us

profile of v2, /device:TPU:1, one launch (start us, length us, event | category | flops | bytes accessed | tf_op | source)
XLA Modules:
  0.0 77.8 jit_solution(11332638188186839844)
XLA Ops:
  0.7 0.7 convert_bitcast_fusion
  1.4 0.1 copy.14
  1.5 0.8 %reshape.8.weight_ref = f32[432]{0:T(512)} reshape(f32[3,3,16,3]{3,2,1,0:T(8,128)S(1)} %copy.14) | data formatting | bytes 3456 | tf_op jit(solution)/shard_map/reshape | solution.py:529
  2.3 73.4 %spectral.1 = bf16[3,2,16,4096]{3,2,1,0:T(8,128)(2,1)} custom-call(f32[432]{0:T(512)} %reshape.8.weight_ref, f32[3]{0:T(128)} %bias_ref.1, f32[3]{0:T(128)} %wave_ref.1, f32[1]{0:T(128)S(6)} %copy.16.travel_ref, bf16[16,256,256]{2,1,0:T(8,128)(2,1)} %features_ref.1, bf16[2,512,512]{2,1,0:T(8,128)(2,1)} %constant.16.clone.forward_ref, ...), custom_call_target="tpu_custom_call" | custom-call | tf_op jit(solution)/shard_map/spectral/pallas_call | solution.py:533
  75.7 2.1 %copy.17 = bf16[3,2,16,4096]{3,2,1,0:T(8,128)(2,1)} copy(bf16[3,2,16,4096]{3,2,1,0:T(8,128)(2,1)} %spectral.1) | data formatting | bytes 1572864

commit v3 on v2

--- a/solution.py
+++ b/solution.py
@@ -29,18 +29,14 @@
     b = np.arange(256)
     rot = rotation_np(2.0 * np.pi * ((k2[:, None] * b[None, :]) % 256) / 256.0)
     forward_y = rot.reshape(2, 2, 64, 4, 256).transpose(2, 0, 3, 1, 4).reshape(512, 512)
-    inverse_y = forward_y.T
     j = np.arange(16)
     rot16 = rotation_np(2.0 * np.pi * ((j[:, None] * j[None, :]) % 16) / 16.0)
     back16 = np.stack([np.stack([rot16[0, 0], -rot16[0, 1]]), np.stack([-rot16[1, 0], rot16[1, 1]])])
-    spread16 = np.einsum("pqjk,rs->pjrqks", back16, np.eye(16)).reshape(512, 512)
     lanes = np.einsum("pqab,cd->qcbpda", rot16, np.eye(8)).reshape(256, 256)
     lanes_back = np.einsum("pqab,cd->qcbpda", back16, np.eye(8)).reshape(256, 256)
     k1 = np.arange(16)
     angle = 2.0 * np.pi * ((k1[:, None] * b[None, :]) % 4096) / 4096.0
     twist_y = np.stack([np.cos(angle), -np.sin(angle)]).astype(np.float32)
-    twist_back = np.stack([np.cos(angle.T), np.sin(angle.T)])
-    twist_back = np.repeat(twist_back, 16, axis=2).astype(np.float32)
     p = np.arange(128).reshape(64, 2)
     r = np.arange(16)
     angle = 2.0 * np.pi * ((p[:, :, None] * r) % 2048) / 2048.0
@@ -49,12 +45,9 @@
     twist_x = twist_x.reshape(2, 64, 8, 128).astype(np.float32)
     return {
         "forward_y": split_np(forward_y * 8.0),
-        "inverse_y": split_np(inverse_y * 2.0**-10),
-        "spread16": split_np(spread16),
         "lanes": split_np(lanes),
         "lanes_back": split_np(lanes_back * 2.0**-16),
         "twist_y": twist_y,
-        "twist_back": twist_back,
         "twist_x": twist_x,
     }
 
@@ -149,60 +142,36 @@
 
 NN = ((1,), (0,))
 NT = ((1,), (1,))
+TN = ((0,), (0,))
 
 
 LOGICAL = pl.DeviceIdType.LOGICAL
 
 
-def enter(me, free, members):
+def enter(i, j):
     barrier = pltpu.get_barrier_semaphore()
-    row, col = me // members, me % members
-    rows = 128 // members
-
-    def signal(sem, device):
-        pl.semaphore_signal(sem, inc=1, device_id=device, device_id_type=LOGICAL)
-
-    def up():
-        @pl.when(row > 0)
-        def _():
-            signal(barrier, col)
+
+    def signal(row, col):
+        pl.semaphore_signal(barrier, inc=1, device_id=row * 16 + col, device_id_type=LOGICAL)
+
+    for step in range(1, 16):
+        signal(i, (j + step) % 16)
+    for step in range(1, 8):
+        signal((i + step) % 8, j)
+    for row in (7, 1):
+        for col in (15, 1):
+            signal((i + row) % 8, (j + col) % 16)
 
     def down():
-        @pl.when(row > 0)
-        def _():
-            pl.semaphore_wait(free, 1)
-
-        @pl.when((row == 0) & (col > 0))
-        def _():
-            pl.semaphore_wait(barrier, rows - 1)
-            signal(barrier, 0)
-            pl.semaphore_wait(free, 1)
-
-        @pl.when(me == 0)
-        def _():
-            pl.semaphore_wait(barrier, rows - 1 + members - 1)
-
-            def tell(k, carry):
-                signal(free, k)
-                return carry
-
-            lax.fori_loop(1, members, tell, 0)
-
-        @pl.when(row == 0)
-        def _():
-            def tell(k, carry):
-                signal(free, k * members + col)
-                return carry
-
-            lax.fori_loop(1, rows, tell, 0)
-
-    return up, down
+        pl.semaphore_wait(barrier, 26)
+
+    return down
 
 
 def send_all(me, block_of, landing, send_sem, recv_sem, local_sem):
     pltpu.make_async_copy(block_of(me), landing.at[me], local_sem).start()
 
-    def step(k, carry):
+    def one(k):
         peer = (me + k) % 128
         pltpu.make_async_remote_copy(
             src_ref=block_of(peer),
@@ -212,9 +181,15 @@
             device_id=peer,
             device_id_type=LOGICAL,
         ).start()
+
+    def group(g, carry):
+        for k in range(8):
+            one(8 * g + k)
         return carry
 
-    lax.fori_loop(1, 128, step, 0)
+    for k in range(1, 8):
+        one(k)
+    lax.fori_loop(1, 16, group, 0)
 
 
 def wait_all(landing, send_sem, recv_sem, local_sem):
@@ -338,19 +313,26 @@
             out_ref[s + 64, o] = encode(total - delta)
 
 
-def rows_inverse(o, in_ref, matrix_ref, twist_ref, spread_ref, out_ref):
-    left = decode(in_ref[:, 0, o]).reshape(512, 128)
-    right = decode(in_ref[:, 1, o]).reshape(512, 128)
-    data = split(jnp.concatenate([left, right], axis=1))
-    value = dot3((matrix_ref[0], matrix_ref[1]), data, NN)
-    re, im = value[:256], value[256:]
-    c, s = twist_ref[0], twist_ref[1]
-    value = jnp.concatenate([re * c - im * s, re * s + im * c], axis=1)
-    result = dot3((spread_ref[0], spread_ref[1]), split(value), NT)
-    for part in range(2):
-        for j in range(16):
-            rows = result[part * 256 + j * 16 : part * 256 + j * 16 + 16, :]
-            out_ref[o, part, :, j * 256 : (j + 1) * 256] = rows.astype(BF16)
+def rows_inverse(o, in_ref, matrix_ref, twist_ref, value_ref, out_ref):
+    for h in range(2):
+        hi, lo = split(decode(in_ref[:, h, o]).reshape(512, 128))
+        rows = pl.ds(h * 128, 128)
+        value_ref[rows, :] = dot3((hi, lo), (matrix_ref[0], matrix_ref[1]), TN)
+    for half in range(2):
+        cols = pl.ds(half * 128, 128)
+        spectrum = []
+        for k1 in range(16):
+            rows = pl.ds(k1 * 16, 16)
+            re = value_ref[rows, cols] * 2.0**-13
+            im = value_ref[rows, pl.ds(256 + half * 128, 128)] * 2.0**-13
+            if k1 > 0:
+                c = twist_ref[0, pl.ds(k1, 1), cols]
+                s = twist_ref[1, pl.ds(k1, 1), cols]
+                re, im = re * c + im * s, im * c - re * s
+            spectrum.append((re, im))
+        for j, field in enumerate(fft16(spectrum, 1.0)):
+            for part in range(2):
+                out_ref[o, part, :, pl.ds(j * 256 + half * 128, 128)] = field[part].astype(BF16)
 
 
 def band(weight_ref, band_ref):
@@ -358,33 +340,30 @@
     lane = lax.broadcasted_iota(jnp.int32, (32, 128), 1)
     shift = lane % 64 - x - 15
     upper = lane < 64
-
-    def block(vo, carry):
-        for pair in range(8):
-            value = jnp.zeros((32, 128), F32)
-            for u in range(3):
-                base = (vo * 16 + 2 * pair) * 3 + u
-                both = jnp.where(upper, weight_ref[base], weight_ref[base + 3])
-                value = jnp.where(shift == u, both, value)
-            band_ref[pl.ds(pl.multiple_of(vo * 32, 32), 32), pair * 128 : (pair + 1) * 128] = value.astype(BF16)
-        return carry
-
-    lax.fori_loop(0, 9, block, 0)
     row = lax.broadcasted_iota(jnp.int32, (16, 128), 0)
-    lane = lax.broadcasted_iota(jnp.int32, (16, 128), 1)
-    upper = lane < 64
-    for place, (source, u) in enumerate(((16, 2), (47, 0))):
-        here = lane % 64 == source
-        for pair in range(8):
-            value = jnp.zeros((16, 128), F32)
-            for vo in range(9):
-                base = (vo * 16 + 2 * pair) * 3 + u
-                both = jnp.where(upper, weight_ref[base], weight_ref[base + 3])
-                value = jnp.where(here & (row == vo), both, value)
-            band_ref[288 + 16 * place : 304 + 16 * place, pair * 128 : (pair + 1) * 128] = value.astype(BF16)
-
-
-def head(i, j, weight_ref, bias_ref, band_ref, tile_ref, sums_ref, sides_ref, edges_ref, got_sides_ref, got_edges_ref, phase_ref, down, border_sems, send_phase):
+    beyond = [(lane[:16] % 64 == source, u) for source, u in ((16, 2), (47, 0))]
+    for pair in range(8):
+        columns_of = pl.ds(pair * 128, 128)
+        edges = [jnp.zeros((16, 128), F32), jnp.zeros((16, 128), F32)]
+        for o in range(3):
+            low = weight_ref[o, 2 * pair].astype(F32)
+            high = weight_ref[o, 2 * pair + 1].astype(F32)
+            for v in range(3):
+                value = jnp.zeros((32, 128), F32)
+                for u in range(3):
+                    a = jnp.broadcast_to(low[u : u + 1, v : v + 1], (32, 128))
+                    b = jnp.broadcast_to(high[u : u + 1, v : v + 1], (32, 128))
+                    both = jnp.where(upper, a, b)
+                    value = jnp.where(shift == u, both, value)
+                    for n, (here, edge_u) in enumerate(beyond):
+                        if u == edge_u:
+                            edges[n] = jnp.where(here & (row == v * 3 + o), both[:16], edges[n])
+                band_ref[(v * 3 + o) * 32 : (v * 3 + o) * 32 + 32, columns_of] = value.astype(BF16)
+        for n in range(2):
+            band_ref[288 + 16 * n : 304 + 16 * n, columns_of] = edges[n].astype(BF16)
+
+
+def head(i, j, weight_ref, bias_ref, band_ref, tile_ref, sums_ref, sides_ref, edges_ref, got_sides_ref, got_edges_ref, phase_ref, down, border_sems, send_phase, meanwhile):
     band(weight_ref, band_ref)
     lane = lax.broadcasted_iota(jnp.int32, (32, 128), 1)
     to_right = jnp.zeros((32, 128), F32)
@@ -420,6 +399,7 @@
     ]
     for copy in copies:
         copy.start()
+    meanwhile()
     for copy in copies:
         copy.wait()
     below, above = i < 7, i > 0
@@ -465,22 +445,28 @@
 
 def spectral_kernel(
     weight_ref, bias_ref, wave_ref, travel_ref, features_ref,
-    forward_ref, inverse_ref, spread_ref, lanes_ref, back_ref, twist_y_ref, twist_back_ref, twist_x_ref,
+    forward_ref, lanes_ref, back_ref, twist_y_ref, twist_x_ref,
     out_ref,
     tile_ref, band_ref, sums_ref, sides_ref, edges_ref, got_sides_ref, got_edges_ref, phase_ref, got_phase_ref,
-    packets_ref, spread_in_ref, filtered_ref, returned_ref, cos_ref, sin_ref, re_ref, im_ref, hi_ref, lo_ref, field_hi_ref, field_lo_ref,
-    free_sem, tile_sem, border_send, border_recv, send_sems, recv_sems, local_sems,
+    packets_ref, spread_in_ref, filtered_ref, returned_ref, cos_ref, sin_ref, re_ref, im_ref, hi_ref, lo_ref, field_hi_ref, field_lo_ref, value_ref,
+    tile_sem, border_send, border_recv, send_sems, recv_sems, local_sems,
 ):
     colors = 3
     i, j = lax.axis_index("row"), lax.axis_index("col")
     me = i * 16 + j
-    up, down = enter(me, free_sem, 16)
-    up()
+    down = enter(i, j)
     load = pltpu.make_async_copy(features_ref, tile_ref.at[:, pl.ds(16, 256), :], tile_sem)
     load.start()
     tile_ref[:, 0:16, :] = jnp.zeros((16, 16, 256), BF16)
     tile_ref[:, 272:288, :] = jnp.zeros((16, 16, 256), BF16)
     load.wait()
+
+    def each(body):
+        def step(o, carry):
+            body(o)
+            return carry
+
+        lax.fori_loop(0, colors, step, 0)
 
     def send_phase(peer):
         @pl.when(peer == j)
@@ -497,18 +483,11 @@
     head(
         i, j, weight_ref, bias_ref, band_ref, tile_ref, sums_ref, sides_ref, edges_ref, got_sides_ref, got_edges_ref, phase_ref,
         down, (border_send, border_recv), send_phase,
+        lambda: each(lambda o: transfer(o, me, wave_ref[o], travel_ref[0], cos_ref, sin_ref)),
     )
-
-    def each(body):
-        def step(o, carry):
-            body(o)
-            return carry
-
-        lax.fori_loop(0, colors, step, 0)
 
     first = (send_sems.at[0], recv_sems.at[0], local_sems.at[0])
     second = (send_sems.at[1], recv_sems.at[1], local_sems.at[1])
-    each(lambda o: transfer(o, me, wave_ref[o], travel_ref[0], cos_ref, sin_ref))
     wait_all(got_phase_ref, send_sems.at[2], recv_sems.at[2], local_sems.at[2])
     by_pair = packets_ref.reshape(64, 2, colors, 8, 128)
     each(lambda o: rows_forward(o, got_phase_ref, forward_ref, twist_y_ref, by_pair, field_hi_ref, field_lo_ref))
@@ -518,21 +497,20 @@
     send_all(me, lambda d: filtered_ref.at[d], returned_ref, *second)
     wait_all(returned_ref, *second)
     by_pair_back = returned_ref.reshape(64, 2, colors, 8, 128)
-    each(lambda o: rows_inverse(o, by_pair_back, inverse_ref, twist_back_ref, spread_ref, out_ref))
+    each(lambda o: rows_inverse(o, by_pair_back, forward_ref, twist_y_ref, value_ref, out_ref))
 
 
 def per_device(features, conv_weight, bias, wave, travel):
     table = tables()
     colors = 3
-    names = ("forward_y", "inverse_y", "spread16", "lanes", "lanes_back", "twist_y", "twist_back", "twist_x")
+    names = ("forward_y", "lanes", "lanes_back", "twist_y", "twist_x")
     args = [jnp.asarray(table[k]) for k in names]
-    weight = conv_weight.astype(F32).transpose(3, 0, 1, 2).reshape(-1)
     smem = pl.BlockSpec(memory_space=pltpu.SMEM)
     vmem = pl.BlockSpec(memory_space=pltpu.VMEM)
     exchange = pltpu.VMEM((128, colors, 8, 128), BF16)
     return pl.pallas_call(
         spectral_kernel,
-        in_specs=[smem] * 4 + [pl.BlockSpec(memory_space=pl.ANY)] + [vmem] * len(args),
+        in_specs=[vmem] + [smem] * 3 + [pl.BlockSpec(memory_space=pl.ANY)] + [vmem] * len(args),
         out_specs=vmem,
         out_shape=jax.ShapeDtypeStruct((colors, 2, 16, 4096), BF16),
         scratch_shapes=[
@@ -554,7 +532,7 @@
             pltpu.VMEM((64, 8, 256), BF16),
             pltpu.VMEM((256, 512), BF16),
             pltpu.VMEM((256, 512), BF16),
-            pltpu.SemaphoreType.REGULAR,
+            pltpu.VMEM((256, 512), F32),
             pltpu.SemaphoreType.DMA,
             pltpu.SemaphoreType.DMA((8,)),
             pltpu.SemaphoreType.DMA((8,)),
@@ -564,7 +542,7 @@
         ],
         compiler_params=pltpu.CompilerParams(collective_id=0, has_side_effects=True, vmem_limit_bytes=VMEM_LIMIT),
         name="spectral",
-    )(weight, bias, wave, travel, features, *args)
+    )(conv_weight, bias, wave, travel, features, *args)
 
 
 def solution(mesh):

time: 78.2 us -> 68.9 us (0.88)
  Pallas kernels: 73.4 us -> 64.5 us
    pallas_call x1, Pallas kernels: 73.4 us -> 64.5 us  [per_device(): pl.pallas_call(spectral_kernel, in_specs=[vmem] + [smem] * 3 + [pl.BlockS...]
    unnamed x1 -> x2, local copies, waits for them, and re-layouts: 2.06 us -> 3.52 us
    reshape x2 -> x0, local copies, waits for them, and re-layouts: 0.92 us -> none  [per_device(): weight = conv_weight.astype(F32).transpose(3, 0, 1, 2).reshape(-1)]
where the time goes in v3:
time: 68.9 us; the launch traced here: 68.7 us
  Pallas kernels  64.5 us (94%)
  local copies, waits for them, and re-layouts  3.52 us (5%)
    pallas_call x1, Pallas kernels, per_device(): pl.pallas_call(spectral_kernel, in_specs=[vmem] + [smem] * 3 + [pl.BlockS...  64.5 us
    unnamed x2, local copies, waits for them, and re-layouts  3.52 us

profile of v3, /device:TPU:1, one launch (start us, length us, event | category | flops | bytes accessed | tf_op | source)
XLA Modules:
  0.0 68.7 jit_solution(9966525494297280067)
XLA Ops:
  0.7 1.5 %copy.11.weight_ref = bf16[3,16,3,3]{3,2,1,0:T(4,128)(2,1)} copy(bf16[3,16,3,3]{1,3,2,0:T(4,128)(2,1)} %param.11) | data formatting | bytes 1728 | tf_op args[1]
  2.1 64.5 %spectral.1 = bf16[3,2,16,4096]{3,2,1,0:T(8,128)(2,1)} custom-call(bf16[3,16,3,3]{3,2,1,0:T(4,128)(2,1)} %copy.11.weight_ref, f32[3]{0:T(128)} %bias_ref.1, f32[3]{0:T(128)} %wave_ref.1, f32[1]{0:T(128)S(6)} %copy.13.travel_ref, bf16[16,256,256]{2,1,0:T(8,128)(2,1)} %features_ref.1, bf16[2,512,512]{2,1,0:T(8,128)(2,1)} %constant.10.clone.forward_ref, ...), custom_call_target="tpu_custom_call" | custom-call | tf_op jit(solution)/shard_map/spectral/pallas_call | solution.py:511
  66.6 2.1 %copy.14 = bf16[3,2,16,4096]{3,2,1,0:T(8,128)(2,1)} copy(bf16[3,2,16,4096]{3,2,1,0:T(8,128)(2,1)} %spectral.1) | data formatting | bytes 1572864

commit v4 on v3

--- a/solution.py
+++ b/solution.py
@@ -61,7 +61,7 @@
 
 def decode(y):
     y = y.astype(F32)
-    root = jnp.sqrt(jnp.sqrt(jnp.sqrt(jnp.abs(y))))
+    root = jnp.exp2(jnp.log2(jnp.abs(y)) * 0.125)
     return jnp.where(y < 0.0, -root, root)
 
 
@@ -204,7 +204,7 @@
         cols = pl.ds(half * 128, 128)
         field = []
         for j in range(16):
-            field.append(cos_sin_quarters(2.0 * decode(phase_ref[j, o, :, cols])))
+            field.append(cos_sin_quarters(2.0 * decode(phase_ref[o, j, :, cols])))
         spectrum = fft16(field, -1.0)
         for k1 in range(16):
             re, im = spectrum[k1]
@@ -313,7 +313,7 @@
             out_ref[s + 64, o] = encode(total - delta)
 
 
-def rows_inverse(o, in_ref, matrix_ref, twist_ref, value_ref, out_ref):
+def rows_inverse(o, in_ref, matrix_ref, twist_ref, out_ref, value_ref):
     for h in range(2):
         hi, lo = split(decode(in_ref[:, h, o]).reshape(512, 128))
         rows = pl.ds(h * 128, 128)
@@ -335,6 +335,9 @@
                 out_ref[o, part, :, pl.ds(j * 256 + half * 128, 128)] = field[part].astype(BF16)
 
 
+EDGE_ROW = (0, 6, 3)
+
+
 def band(weight_ref, band_ref):
     x = lax.broadcasted_iota(jnp.int32, (32, 128), 0)
     lane = lax.broadcasted_iota(jnp.int32, (32, 128), 1)
@@ -346,24 +349,24 @@
         columns_of = pl.ds(pair * 128, 128)
         edges = [jnp.zeros((16, 128), F32), jnp.zeros((16, 128), F32)]
         for o in range(3):
-            low = weight_ref[o, 2 * pair].astype(F32)
-            high = weight_ref[o, 2 * pair + 1].astype(F32)
+            weights = [weight_ref[o, u].astype(F32) for u in range(3)]
             for v in range(3):
                 value = jnp.zeros((32, 128), F32)
                 for u in range(3):
-                    a = jnp.broadcast_to(low[u : u + 1, v : v + 1], (32, 128))
-                    b = jnp.broadcast_to(high[u : u + 1, v : v + 1], (32, 128))
+                    c = 2 * pair
+                    a = jnp.broadcast_to(weights[u][v : v + 1, c : c + 1], (32, 128))
+                    b = jnp.broadcast_to(weights[u][v : v + 1, c + 1 : c + 2], (32, 128))
                     both = jnp.where(upper, a, b)
                     value = jnp.where(shift == u, both, value)
                     for n, (here, edge_u) in enumerate(beyond):
                         if u == edge_u:
-                            edges[n] = jnp.where(here & (row == v * 3 + o), both[:16], edges[n])
+                            edges[n] = jnp.where(here & (row == EDGE_ROW[v] + o), both[:16], edges[n])
                 band_ref[(v * 3 + o) * 32 : (v * 3 + o) * 32 + 32, columns_of] = value.astype(BF16)
         for n in range(2):
             band_ref[288 + 16 * n : 304 + 16 * n, columns_of] = edges[n].astype(BF16)
 
 
-def head(i, j, weight_ref, bias_ref, band_ref, tile_ref, sums_ref, sides_ref, edges_ref, got_sides_ref, got_edges_ref, phase_ref, down, border_sems, send_phase, meanwhile):
+def head(i, j, weight_ref, bias_ref, band_ref, tile_ref, sums_ref, sides_ref, edges_ref, got_sides_ref, got_edges_ref, got_corners_ref, phase_ref, down, border_sems, send_phase, meanwhile):
     band(weight_ref, band_ref)
     lane = lax.broadcasted_iota(jnp.int32, (32, 128), 1)
     to_right = jnp.zeros((32, 128), F32)
@@ -388,8 +391,11 @@
     for slot, step in enumerate((1, -1)):
         copies.append((sides_ref.at[slot], got_sides_ref.at[slot], i, (j + step + 16) % 16))
     for edge, down_step in enumerate((-1, 1)):
-        for side, step in enumerate((-1, 0, 1)):
-            copies.append((edges_ref.at[edge], got_edges_ref.at[edge * 3 + 2 - side], (i + down_step + 8) % 8, (j + step + 16) % 16))
+        row = (i + down_step + 8) % 8
+        copies.append((edges_ref.at[edge], got_edges_ref.at[edge], row, j))
+        for side, step in enumerate((1, -1)):
+            corner = edges_ref.at[edge, pl.ds(0, 8), pl.ds(128 * (1 - side), 128)]
+            copies.append((corner, got_corners_ref.at[edge * 2 + side], row, (j + step + 16) % 16))
     copies = [
         pltpu.make_async_remote_copy(
             src_ref=source, dst_ref=target, send_sem=send_sems.at[n], recv_sem=recv_sems.at[n],
@@ -407,11 +413,12 @@
     wide = lax.broadcasted_iota(jnp.int32, (32, 256), 1)
     tall = lax.broadcasted_iota(jnp.int32, (32, 1), 0)
 
-    def rows_beyond(k, vo):
+    def rows_beyond(k, v, o):
         first = (tall == 0) & (k == 0) & above
         last = (tall == 31) & (k == 7) & below
-        top = got_edges_ref[4, vo : vo + 1, :]
-        bottom = got_edges_ref[1, vo : vo + 1, :]
+        place = pl.ds(EDGE_ROW[v] + o, 1)
+        top = got_edges_ref[1, place, :]
+        bottom = got_edges_ref[0, place, :]
         return jnp.where(first, top, jnp.where(last, bottom, 0.0))
 
     def column_beyond(k, o, side):
@@ -419,37 +426,39 @@
         value = jnp.sum(jnp.where(lane == 3 * k + o, sides, 0.0), axis=1, keepdims=True)
         first = (tall == 0) & (k == 0) & above
         last = (tall == 31) & (k == 7) & below
-        vo, y = (o, 255) if side == 0 else (6 + o, 0)
-        top = got_edges_ref[3 + 2 * side, vo : vo + 1, y : y + 1]
-        bottom = got_edges_ref[2 * side, vo : vo + 1, y : y + 1]
+        place, y = pl.ds(EDGE_ROW[2 * side] + o, 1), 127 * (1 - side)
+        top = got_corners_ref[2 + side, place, :][:, y : y + 1]
+        bottom = got_corners_ref[side, place, :][:, y : y + 1]
         value = value + jnp.where(first, top, jnp.where(last, bottom, 0.0))
         return jnp.where(left if side == 0 else right, value, 0.0)
 
-    def block(step, carry):
-        k = (j // 2 + step) % 8
-        for o in range(3):
-            first = sums_ref[k, o] + rows_beyond(k, o)
-            middle = sums_ref[k, 3 + o] + rows_beyond(k, 3 + o)
-            last = sums_ref[k, 6 + o] + rows_beyond(k, 6 + o)
+    for o in range(3):
+
+        def block(step, carry):
+            k = (j // 2 + step) % 8
+            first = sums_ref[k, o] + rows_beyond(k, 0, o)
+            middle = sums_ref[k, 3 + o] + rows_beyond(k, 1, o)
+            last = sums_ref[k, 6 + o] + rows_beyond(k, 2, o)
             first = jnp.where(wide == 0, column_beyond(k, o, 0), pltpu.roll(first, 1, 1))
             last = jnp.where(wide == 255, column_beyond(k, o, 1), pltpu.roll(last, 255, 1))
             value = encode(jnp.tanh(first + middle + last + bias_ref[o]))
-            phase_ref[2 * k, o] = value[:16]
-            phase_ref[2 * k + 1, o] = value[16:]
-        send_phase(2 * k)
-        send_phase(2 * k + 1)
-        return carry
-
-    lax.fori_loop(0, 8, block, 0)
+            phase_ref[o, 2 * k] = value[:16]
+            phase_ref[o, 2 * k + 1] = value[16:]
+            send_phase(o, 2 * k)
+            send_phase(o, 2 * k + 1)
+            return carry
+
+        lax.fori_loop(0, 8, block, 0)
 
 
 def spectral_kernel(
     weight_ref, bias_ref, wave_ref, travel_ref, features_ref,
-    forward_ref, lanes_ref, back_ref, twist_y_ref, twist_x_ref,
-    out_ref,
-    tile_ref, band_ref, sums_ref, sides_ref, edges_ref, got_sides_ref, got_edges_ref, phase_ref, got_phase_ref,
-    packets_ref, spread_in_ref, filtered_ref, returned_ref, cos_ref, sin_ref, re_ref, im_ref, hi_ref, lo_ref, field_hi_ref, field_lo_ref, value_ref,
-    tile_sem, border_send, border_recv, send_sems, recv_sems, local_sems,
+    forward_hbm, lanes_hbm, back_hbm, twist_x_hbm, twist_y_ref,
+    returned_ref,
+    forward_ref, lanes_ref, back_ref, twist_x_ref,
+    tile_ref, band_ref, sums_ref, sides_ref, edges_ref, got_sides_ref, got_edges_ref, got_corners_ref, phase_ref, got_phase_ref,
+    packets_ref, spread_in_ref, filtered_ref, cos_ref, sin_ref, re_ref, im_ref, hi_ref, lo_ref, field_hi_ref, field_lo_ref,
+    tile_sem, table_sems, border_send, border_recv, send_sems, recv_sems, local_sems,
 ):
     colors = 3
     i, j = lax.axis_index("row"), lax.axis_index("col")
@@ -457,6 +466,10 @@
     down = enter(i, j)
     load = pltpu.make_async_copy(features_ref, tile_ref.at[:, pl.ds(16, 256), :], tile_sem)
     load.start()
+    tables_in = []
+    for n, (source, target) in enumerate(((forward_hbm, forward_ref), (lanes_hbm, lanes_ref), (back_hbm, back_ref), (twist_x_hbm, twist_x_ref))):
+        tables_in.append(pltpu.make_async_copy(source, target, table_sems.at[n]))
+        tables_in[n].start()
     tile_ref[:, 0:16, :] = jnp.zeros((16, 16, 256), BF16)
     tile_ref[:, 272:288, :] = jnp.zeros((16, 16, 256), BF16)
     load.wait()
@@ -468,62 +481,85 @@
 
         lax.fori_loop(0, colors, step, 0)
 
-    def send_phase(peer):
+    def send_phase(o, peer):
+        n = 2 + o
+
         @pl.when(peer == j)
         def _():
-            pltpu.make_async_copy(phase_ref.at[peer], got_phase_ref.at[j], local_sems.at[2]).start()
+            pltpu.make_async_copy(phase_ref.at[o, peer], got_phase_ref.at[o, j], local_sems.at[n]).start()
 
         @pl.when(peer != j)
         def _():
             pltpu.make_async_remote_copy(
-                src_ref=phase_ref.at[peer], dst_ref=got_phase_ref.at[j], send_sem=send_sems.at[2], recv_sem=recv_sems.at[2],
+                src_ref=phase_ref.at[o, peer], dst_ref=got_phase_ref.at[o, j], send_sem=send_sems.at[n], recv_sem=recv_sems.at[n],
                 device_id=i * 16 + peer, device_id_type=LOGICAL,
             ).start()
 
     head(
-        i, j, weight_ref, bias_ref, band_ref, tile_ref, sums_ref, sides_ref, edges_ref, got_sides_ref, got_edges_ref, phase_ref,
+        i, j, weight_ref, bias_ref, band_ref, tile_ref, sums_ref, sides_ref, edges_ref, got_sides_ref, got_edges_ref, got_corners_ref, phase_ref,
         down, (border_send, border_recv), send_phase,
         lambda: each(lambda o: transfer(o, me, wave_ref[o], travel_ref[0], cos_ref, sin_ref)),
     )
 
     first = (send_sems.at[0], recv_sems.at[0], local_sems.at[0])
     second = (send_sems.at[1], recv_sems.at[1], local_sems.at[1])
-    wait_all(got_phase_ref, send_sems.at[2], recv_sems.at[2], local_sems.at[2])
     by_pair = packets_ref.reshape(64, 2, colors, 8, 128)
-    each(lambda o: rows_forward(o, got_phase_ref, forward_ref, twist_y_ref, by_pair, field_hi_ref, field_lo_ref))
+
+    def forward(o):
+        wait_all(got_phase_ref.at[o], send_sems.at[2 + o], recv_sems.at[2 + o], local_sems.at[2 + o])
+        rows_forward(o, got_phase_ref, forward_ref, twist_y_ref, by_pair, field_hi_ref, field_lo_ref)
+
+    tables_in[0].wait()
+    each(forward)
     send_all(me, lambda d: packets_ref.at[d], spread_in_ref, *first)
+    for table in tables_in[1:]:
+        table.wait()
     wait_all(spread_in_ref, *first)
     each(lambda o: columns(o, spread_in_ref, lanes_ref, back_ref, twist_x_ref, cos_ref, sin_ref, filtered_ref, re_ref, im_ref, hi_ref, lo_ref))
     send_all(me, lambda d: filtered_ref.at[d], returned_ref, *second)
     wait_all(returned_ref, *second)
-    by_pair_back = returned_ref.reshape(64, 2, colors, 8, 128)
-    each(lambda o: rows_inverse(o, by_pair_back, forward_ref, twist_y_ref, value_ref, out_ref))
+
+
+def rows_inverse_kernel(returned_ref, matrix_ref, twist_ref, out_ref, value_ref, result_ref, sems):
+    colors = result_ref.shape[0]
+    by_pair = returned_ref.reshape(64, 2, colors, 8, 128)
+
+    def step(o, carry):
+        rows_inverse(o, by_pair, matrix_ref, twist_ref, result_ref, value_ref)
+        pltpu.make_async_copy(result_ref.at[o], out_ref.at[o], sems.at[o]).start()
+        return carry
+
+    lax.fori_loop(0, colors, step, 0)
+    for o in range(colors):
+        pltpu.make_async_copy(result_ref.at[o], out_ref.at[o], sems.at[o]).wait()
 
 
 def per_device(features, conv_weight, bias, wave, travel):
     table = tables()
     colors = 3
-    names = ("forward_y", "lanes", "lanes_back", "twist_y", "twist_x")
+    names = ("forward_y", "lanes", "lanes_back", "twist_x", "twist_y")
     args = [jnp.asarray(table[k]) for k in names]
     smem = pl.BlockSpec(memory_space=pltpu.SMEM)
     vmem = pl.BlockSpec(memory_space=pltpu.VMEM)
     exchange = pltpu.VMEM((128, colors, 8, 128), BF16)
-    return pl.pallas_call(
+    returned = pl.pallas_call(
         spectral_kernel,
-        in_specs=[vmem] + [smem] * 3 + [pl.BlockSpec(memory_space=pl.ANY)] + [vmem] * len(args),
+        in_specs=[vmem] + [smem] * 3 + [pl.BlockSpec(memory_space=pl.ANY)] * 5 + [vmem],
         out_specs=vmem,
-        out_shape=jax.ShapeDtypeStruct((colors, 2, 16, 4096), BF16),
+        out_shape=pltpu.VMEM((128, colors, 8, 128), BF16),
         scratch_shapes=[
+            *(pltpu.VMEM(a.shape, a.dtype) for a in args[:4]),
             pltpu.VMEM((16, 288, 256), BF16),
             pltpu.VMEM((320, 1024), BF16),
             pltpu.VMEM((8, 9, 32, 256), F32),
             pltpu.VMEM((2, 32, 128), F32),
             pltpu.VMEM((2, 16, 256), F32),
             pltpu.VMEM((2, 32, 128), F32),
-            pltpu.VMEM((6, 16, 256), F32),
-            pltpu.VMEM((16, colors, 16, 256), BF16),
-            pltpu.VMEM((16, colors, 16, 256), BF16),
-            exchange, exchange, exchange, exchange,
+            pltpu.VMEM((2, 16, 256), F32),
+            pltpu.VMEM((4, 8, 128), F32),
+            pltpu.VMEM((colors, 16, 16, 256), BF16),
+            pltpu.VMEM((colors, 16, 16, 256), BF16),
+            exchange, exchange, exchange,
             pltpu.VMEM((colors, 64, 8, 128), F32),
             pltpu.VMEM((colors, 64, 8, 128), F32),
             pltpu.VMEM((64, 8, 128), F32),
@@ -532,17 +568,30 @@
             pltpu.VMEM((64, 8, 256), BF16),
             pltpu.VMEM((256, 512), BF16),
             pltpu.VMEM((256, 512), BF16),
-            pltpu.VMEM((256, 512), F32),
             pltpu.SemaphoreType.DMA,
+            pltpu.SemaphoreType.DMA((4,)),
             pltpu.SemaphoreType.DMA((8,)),
             pltpu.SemaphoreType.DMA((8,)),
-            pltpu.SemaphoreType.DMA((3,)),
-            pltpu.SemaphoreType.DMA((3,)),
-            pltpu.SemaphoreType.DMA((3,)),
+            pltpu.SemaphoreType.DMA((5,)),
+            pltpu.SemaphoreType.DMA((5,)),
+            pltpu.SemaphoreType.DMA((5,)),
         ],
         compiler_params=pltpu.CompilerParams(collective_id=0, has_side_effects=True, vmem_limit_bytes=VMEM_LIMIT),
         name="spectral",
-    )(conv_weight, bias, wave, travel, features, *args)
+    )(conv_weight.transpose(0, 2, 3, 1), bias, wave, travel, features, *args)
+    return pl.pallas_call(
+        rows_inverse_kernel,
+        in_specs=[vmem] * 3,
+        out_specs=pl.BlockSpec(memory_space=pl.ANY),
+        out_shape=jax.ShapeDtypeStruct((colors, 2, 16, 4096), BF16),
+        scratch_shapes=[
+            pltpu.VMEM((256, 512), F32),
+            pltpu.VMEM((colors, 2, 16, 4096), BF16),
+            pltpu.SemaphoreType.DMA((colors,)),
+        ],
+        compiler_params=pltpu.CompilerParams(vmem_limit_bytes=16 * 1024 * 1024),
+        name="rows_inverse",
+    )(returned, args[0], args[4])
 
 
 def solution(mesh):

time: 68.9 us -> 61 us (0.89)
  Pallas kernels: 64.5 us -> 60.1 us
  local copies, waits for them, and re-layouts: 3.52 us -> 0.01 us
    pallas_call x1, Pallas kernels: 64.5 us -> 56.9 us  [per_device(): pl.pallas_call(spectral_kernel, in_specs=[vmem] + [smem] * 3 + [pl.BlockS...]
    unnamed x2 -> x4, local copies, waits for them, and re-layouts: 3.52 us -> 0.01 us
    pallas_call x0 -> x1, Pallas kernels: none -> 3.19 us  [per_device(): pl.pallas_call(rows_inverse_kernel, in_specs=[vmem] * 3, out_specs=pl.Blo...]
where the time goes in v4:
time: 61 us; the launch traced here: 60.8 us
  Pallas kernels  60.1 us (99%)
  between operations  0.69 us (1%)
    pallas_call x1, Pallas kernels, per_device(): pl.pallas_call(spectral_kernel, in_specs=[vmem] + [smem] * 3 + [pl.BlockS...  56.9 us
    pallas_call x1, Pallas kernels, per_device(): pl.pallas_call(rows_inverse_kernel, in_specs=[vmem] * 3, out_specs=pl.Blo...  3.19 us

profile of v4, /device:TPU:1, one launch (start us, length us, event | category | flops | bytes accessed | tf_op | source)
XLA Modules:
  0.0 60.8 jit_solution(5835219098478647514)
XLA Ops:
  0.7 0.0 copy-start
  0.7 0.0 copy-start.1
  0.7 56.9 %spectral.1.returned_ref = bf16[128,3,8,128]{3,2,1,0:T(8,128)(2,1)S(1)} custom-call(bf16[3,3,3,16]{3,2,1,0:T(4,128)(2,1)} %bitcast.1, f32[3]{0:T(128)} %bias_ref.1, f32[3]{0:T(128)} %wave_ref.1, f32[1]{0:T(128)S(6)} %copy.11.travel_ref, bf16[16,256,256]{2,1,0:T(8,128)(2,1)} %features_ref.1, bf16[2,512,512]{2,1,0:T(8,128)(2,1)} %constant.10.clone.forward_hbm.matrix_ref, ...), custom_call_target="tpu_custom_call" | custom-call | tf_op jit(solution)/shard_map/spectral/pallas_call | solution.py:545
  57.6 0.0 copy-done
  57.6 0.0 copy-done.1
  57.6 3.2 %rows_inverse.1 = bf16[3,2,16,4096]{3,2,1,0:T(8,128)(2,1)} custom-call(bf16[128,3,8,128]{3,2,1,0:T(8,128)(2,1)S(1)} %spectral.1.returned_ref, bf16[2,512,512]{2,1,0:T(8,128)(2,1)S(1)} %copy-done, f32[2,16,256]{2,1,0:T(8,128)S(1)} %copy-done.1), custom_call_target="tpu_custom_call" | custom-call | tf_op jit(solution)/shard_map/rows_inverse/pallas_call | solution.py:582
Async XLA Ops:
  0.7 56.9 %copy-start = (bf16[2,512,512]{2,1,0:T(8,128)(2,1)S(1)}, bf16[2,512,512]{2,1,0:T(8,128)(2,1)}, u32[]{:S(2)}) copy-start(bf16[2,512,512]{2,1,0:T(8,128)(2,1)} %constant.10.clone.forward_hbm.matrix_ref) | copy-start | bytes 3145732
  0.7 56.9 %copy-start.1 = (f32[2,16,256]{2,1,0:T(8,128)S(1)}, f32[2,16,256]{2,1,0:T(8,128)}, u32[]{:S(2)}) copy-start(f32[2,16,256]{2,1,0:T(8,128)} %constant.14.clone.twist_y_ref.twist_ref) | copy-start | bytes 98308

commit v5 on v4

--- a/solution.py
+++ b/solution.py
@@ -136,8 +136,9 @@
 
 
 def dot3(lhs, rhs, dims):
-    one = functools.partial(lax.dot_general, dimension_numbers=(dims, ((), ())), preferred_element_type=F32)
-    return one(lhs[0], rhs[0]) + (one(lhs[0], rhs[1]) + one(lhs[1], rhs[0]))
+    left = jnp.concatenate([lhs[0], lhs[1], lhs[0]], axis=dims[0][0])
+    right = jnp.concatenate([rhs[0], rhs[0], rhs[1]], axis=dims[1][0])
+    return lax.dot_general(left, right, (dims, ((), ())), preferred_element_type=F32)
 
 
 NN = ((1,), (0,))
@@ -171,8 +172,10 @@
 def send_all(me, block_of, landing, send_sem, recv_sem, local_sem):
     pltpu.make_async_copy(block_of(me), landing.at[me], local_sem).start()
 
+    turn = 1 - 2 * (me % 2)
+
     def one(k):
-        peer = (me + k) % 128
+        peer = (me + turn * (k * 85)) % 128
         pltpu.make_async_remote_copy(
             src_ref=block_of(peer),
             dst_ref=landing.at[me],
@@ -366,9 +369,13 @@
             band_ref[288 + 16 * n : 304 + 16 * n, columns_of] = edges[n].astype(BF16)
 
 
+PHASE_ORDER = ((1, 0), (0, 1), (3, 0), (1, 1), (2, 0), (3, 1), (2, 1), (0, 0))
+
+
 def head(i, j, weight_ref, bias_ref, band_ref, tile_ref, sums_ref, sides_ref, edges_ref, got_sides_ref, got_edges_ref, got_corners_ref, phase_ref, down, border_sems, send_phase, meanwhile):
     band(weight_ref, band_ref)
     lane = lax.broadcasted_iota(jnp.int32, (32, 128), 1)
+    tall = lax.broadcasted_iota(jnp.int32, (32, 128), 0)
     to_right = jnp.zeros((32, 128), F32)
     to_left = jnp.zeros((32, 128), F32)
     for k in range(8):
@@ -411,44 +418,42 @@
     below, above = i < 7, i > 0
     left, right = j > 0, j < 15
     wide = lax.broadcasted_iota(jnp.int32, (32, 256), 1)
-    tall = lax.broadcasted_iota(jnp.int32, (32, 1), 0)
-
-    def rows_beyond(k, v, o):
-        first = (tall == 0) & (k == 0) & above
-        last = (tall == 31) & (k == 7) & below
-        place = pl.ds(EDGE_ROW[v] + o, 1)
-        top = got_edges_ref[1, place, :]
-        bottom = got_edges_ref[0, place, :]
-        return jnp.where(first, top, jnp.where(last, bottom, 0.0))
-
-    def column_beyond(k, o, side):
-        sides = got_sides_ref[side]
-        value = jnp.sum(jnp.where(lane == 3 * k + o, sides, 0.0), axis=1, keepdims=True)
-        first = (tall == 0) & (k == 0) & above
-        last = (tall == 31) & (k == 7) & below
-        place, y = pl.ds(EDGE_ROW[2 * side] + o, 1), 127 * (1 - side)
-        top = got_corners_ref[2 + side, place, :][:, y : y + 1]
-        bottom = got_corners_ref[side, place, :][:, y : y + 1]
-        value = value + jnp.where(first, top, jnp.where(last, bottom, 0.0))
-        return jnp.where(left if side == 0 else right, value, 0.0)
-
+    row = lax.broadcasted_iota(jnp.int32, (8, 256), 0)
+    for edge, (k, rows, here) in enumerate(((7, pl.ds(24, 8), (row == 7) & below), (0, pl.ds(0, 8), (row == 0) & above))):
+        for v in range(3):
+            for o in range(3):
+                beyond = got_edges_ref[edge, pl.ds(EDGE_ROW[v] + o, 1), :]
+                sums_ref[k, v * 3 + o, rows, :] += jnp.where(here, beyond, 0.0)
+    for side, there in enumerate((left, right)):
+        column = got_sides_ref[side]
+        for edge, (k, x, inside) in enumerate(((7, 31, below), (0, 0, above))):
+            corners = got_corners_ref[edge * 2 + side]
+            for o in range(3):
+                y = 127 * (1 - side)
+                corner = corners[EDGE_ROW[2 * side] + o : EDGE_ROW[2 * side] + o + 1, y : y + 1]
+                here = (lane == 3 * k + o) & (tall == x) & inside
+                column = column + jnp.where(here, corner, 0.0)
+        got_sides_ref[side] = jnp.where(there, column, 0.0)
+
+    turn = 1 - 2 * (j % 2)
     for o in range(3):
 
-        def block(step, carry):
-            k = (j // 2 + step) % 8
-            first = sums_ref[k, o] + rows_beyond(k, 0, o)
-            middle = sums_ref[k, 3 + o] + rows_beyond(k, 1, o)
-            last = sums_ref[k, 6 + o] + rows_beyond(k, 2, o)
-            first = jnp.where(wide == 0, column_beyond(k, o, 0), pltpu.roll(first, 1, 1))
-            last = jnp.where(wide == 255, column_beyond(k, o, 1), pltpu.roll(last, 255, 1))
-            value = encode(jnp.tanh(first + middle + last + bias_ref[o]))
+        def block(k):
+            index = 3 * k + o
+            before = pltpu.roll(got_sides_ref[0], 128 - index, 1)
+            after = pltpu.roll(got_sides_ref[1], 127 - index, 1)
+            first = pltpu.roll(sums_ref[k, o], 1, 1)
+            last = pltpu.roll(sums_ref[k, 6 + o], 255, 1)
+            first = jnp.where(wide == 0, jnp.concatenate([before, before], 1), first)
+            last = jnp.where(wide == 255, jnp.concatenate([after, after], 1), last)
+            value = encode(jnp.tanh(first + last + (sums_ref[k, 3 + o] + bias_ref[o])))
             phase_ref[o, 2 * k] = value[:16]
             phase_ref[o, 2 * k + 1] = value[16:]
             send_phase(o, 2 * k)
             send_phase(o, 2 * k + 1)
-            return carry
-
-        lax.fori_loop(0, 8, block, 0)
+
+        for x_step, z_step in PHASE_ORDER:
+            block(((j // 8 + z_step) % 2) * 4 + (j // 2 + turn * x_step) % 4)
 
 
 def spectral_kernel(

time: 61 us -> 59.3 us (0.972)
  Pallas kernels: 60.1 us -> 58.4 us
    pallas_call x1, Pallas kernels: 56.9 us -> 55.3 us  [per_device(): pl.pallas_call(spectral_kernel, in_specs=[vmem] + [smem] * 3 + [pl.BlockS...]
where the time goes in v5:
time: 59.3 us; the launch traced here: 59.2 us
  Pallas kernels  58.4 us (98%)
  between operations  0.69 us (1%)
    pallas_call x1, Pallas kernels, per_device(): pl.pallas_call(spectral_kernel, in_specs=[vmem] + [smem] * 3 + [pl.BlockS...  55.3 us
    pallas_call x1, Pallas kernels, per_device(): pl.pallas_call(rows_inverse_kernel, in_specs=[vmem] * 3, out_specs=pl.Blo...  3.12 us

profile of v5, /device:TPU:1, one launch (start us, length us, event | category | flops | bytes accessed | tf_op | source)
XLA Modules:
  0.0 59.2 jit_solution(2896320520923467529)
XLA Ops:
  0.7 0.0 copy-start
  0.7 0.0 copy-start.1
  0.7 55.3 %spectral.1.returned_ref = bf16[128,3,8,128]{3,2,1,0:T(8,128)(2,1)S(1)} custom-call(bf16[3,3,3,16]{3,2,1,0:T(4,128)(2,1)} %bitcast.1, f32[3]{0:T(128)} %bias_ref.1, f32[3]{0:T(128)} %wave_ref.1, f32[1]{0:T(128)S(6)} %copy.11.travel_ref, bf16[16,256,256]{2,1,0:T(8,128)(2,1)} %features_ref.1, bf16[2,512,512]{2,1,0:T(8,128)(2,1)} %constant.10.clone.forward_hbm.matrix_ref, ...), custom_call_target="tpu_custom_call" | custom-call | tf_op jit(solution)/shard_map/spectral/pallas_call | solution.py:550
  56.0 0.0 copy-done
  56.0 0.0 copy-done.1
  56.0 3.1 %rows_inverse.1 = bf16[3,2,16,4096]{3,2,1,0:T(8,128)(2,1)} custom-call(bf16[128,3,8,128]{3,2,1,0:T(8,128)(2,1)S(1)} %spectral.1.returned_ref, bf16[2,512,512]{2,1,0:T(8,128)(2,1)S(1)} %copy-done, f32[2,16,256]{2,1,0:T(8,128)S(1)} %copy-done.1), custom_call_target="tpu_custom_call" | custom-call | tf_op jit(solution)/shard_map/rows_inverse/pallas_call | solution.py:587
Async XLA Ops:
  0.7 55.4 %copy-start = (bf16[2,512,512]{2,1,0:T(8,128)(2,1)S(1)}, bf16[2,512,512]{2,1,0:T(8,128)(2,1)}, u32[]{:S(2)}) copy-start(bf16[2,512,512]{2,1,0:T(8,128)(2,1)} %constant.10.clone.forward_hbm.matrix_ref) | copy-start | bytes 3145732
  0.7 55.4 %copy-start.1 = (f32[2,16,256]{2,1,0:T(8,128)S(1)}, f32[2,16,256]{2,1,0:T(8,128)}, u32[]{:S(2)}) copy-start(f32[2,16,256]{2,1,0:T(8,128)} %constant.14.clone.twist_y_ref.twist_ref) | copy-start | bytes 98308

commit v6 on v5

--- a/solution.py
+++ b/solution.py
@@ -43,7 +43,13 @@
     twist_x = np.stack([np.cos(angle), -np.sin(angle)])
     twist_x = np.broadcast_to(twist_x[:, :, :, None, None, :], (2, 64, 2, 4, 8, 16))
     twist_x = twist_x.reshape(2, 64, 8, 128).astype(np.float32)
+    s = np.arange(64)
+    pairs = np.stack([np.cos(2.0 * np.pi * s / 128), np.sin(2.0 * np.pi * s / 128)]).astype(np.float32)
+    turn = 2.0 * np.pi * ((s // 8) * (s % 8)) / 64.0
+    turns = np.stack([np.cos(turn), np.sin(turn)]).astype(np.float32)
     return {
+        "pairs": pairs,
+        "turns": turns,
         "forward_y": split_np(forward_y * 8.0),
         "lanes": split_np(lanes),
         "lanes_back": split_np(lanes_back * 2.0**-16),
@@ -169,15 +175,11 @@
     return down
 
 
-def send_all(me, block_of, landing, send_sem, recv_sem, local_sem):
-    pltpu.make_async_copy(block_of(me), landing.at[me], local_sem).start()
-
-    turn = 1 - 2 * (me % 2)
-
-    def one(k):
-        peer = (me + turn * (k * 85)) % 128
+def send_group(c, me, source, landing, send_sem, recv_sem, local_sem):
+    def remote(m):
+        peer = (me + c + 8 * m) % 128
         pltpu.make_async_remote_copy(
-            src_ref=block_of(peer),
+            src_ref=source.at[peer],
             dst_ref=landing.at[me],
             send_sem=send_sem,
             recv_sem=recv_sem,
@@ -185,21 +187,27 @@
             device_id_type=LOGICAL,
         ).start()
 
-    def group(g, carry):
-        for k in range(8):
-            one(8 * g + k)
-        return carry
-
-    for k in range(1, 8):
-        one(k)
-    lax.fori_loop(1, 16, group, 0)
+    @pl.when(c == 0)
+    def _():
+        pltpu.make_async_copy(source.at[me], landing.at[me], local_sem).start()
+
+    @pl.when(c != 0)
+    def _():
+        remote(0)
+
+    for m in range(1, 16):
+        remote(m)
+
+
+def wait_for(refs, sem):
+    pltpu.make_async_copy(refs, refs, sem).wait()
 
 
 def wait_all(landing, send_sem, recv_sem, local_sem):
-    pltpu.make_async_copy(landing.at[0], landing.at[0], local_sem).wait()
     others = landing.at[pl.ds(0, landing.shape[0] - 1)]
-    pltpu.make_async_copy(others, others, send_sem).wait()
-    pltpu.make_async_copy(others, others, recv_sem).wait()
+    wait_for(landing.at[0], local_sem)
+    wait_for(others, send_sem)
+    wait_for(others, recv_sem)
 
 
 def rows_forward(o, phase_ref, matrix_ref, twist_ref, out_ref, hi_ref, lo_ref):
@@ -255,29 +263,29 @@
         lo_ref[place, :, lanes] = lo
 
 
-def columns(o, in_ref, matrix_ref, back_ref, twist_ref, cos_ref, sin_ref, out_ref, re_ref, im_ref, hi_ref, lo_ref):
-    row = lax.broadcasted_iota(jnp.int32, (8, 128), 0)
-    top = row < 4
-    for n2 in range(8):
-        column = []
-        for n1 in range(8):
-            s = 8 * n1 + n2
-            a, b = decode(in_ref[s, o]), decode(in_ref[s + 64, o])
-            total, delta = a + b, a - b
-            re = jnp.where(top, total, pltpu.roll(delta, 4, 0))
-            im = jnp.where(top, pltpu.roll(total, 4, 0), delta)
-            if s > 0:
-                angle = 2.0 * math.pi * s / 128
-                c = jnp.where(top, 1.0, math.cos(angle))
-                w = jnp.where(top, 0.0, math.sin(angle))
-                re, im = re * c + im * w, im * c - re * w
-            column.append((re, im))
-        for m1, v in enumerate(fft8(column, -1.0)):
-            re, im = scaled(v, -2.0 * math.pi * n2 * m1 / 64)
-            re_ref[m1 * 8 + n2] = re
-            im_ref[m1 * 8 + n2] = im
+def columns_in(n2, o, in_ref, pairs_ref, turns_ref, re_ref, im_ref):
+    top = lax.broadcasted_iota(jnp.int32, (8, 128), 0) < 4
+    column = []
+    for n1 in range(8):
+        s = 8 * n1 + n2
+        a, b = decode(in_ref[s, o]), decode(in_ref[s + 64, o])
+        total, delta = a + b, a - b
+        re = jnp.where(top, total, pltpu.roll(delta, 4, 0))
+        im = jnp.where(top, pltpu.roll(total, 4, 0), delta)
+        c = jnp.where(top, 1.0, pairs_ref[0, s])
+        w = jnp.where(top, 0.0, pairs_ref[1, s])
+        column.append((re * c + im * w, im * c - re * w))
+    for m1, (re, im) in enumerate(fft8(column, -1.0)):
+        if m1 > 0:
+            c, w = turns_ref[0, n2 * 8 + m1], turns_ref[1, n2 * 8 + m1]
+            re, im = re * c + im * w, im * c - re * w
+        re_ref[o, m1 * 8 + n2] = re
+        im_ref[o, m1 * 8 + n2] = im
+
+
+def columns(o, matrix_ref, back_ref, twist_ref, cos_ref, sin_ref, re_ref, im_ref, hi_ref, lo_ref):
     for m1 in range(8):
-        column = [(re_ref[m1 * 8 + n2], im_ref[m1 * 8 + n2]) for n2 in range(8)]
+        column = [(re_ref[o, m1 * 8 + n2], im_ref[o, m1 * 8 + n2]) for n2 in range(8)]
         for m2, (re, im) in enumerate(fft8(column, -1.0)):
             place = m1 + 8 * m2
             c, w = twist_ref[0, place], twist_ref[1, place]
@@ -299,26 +307,27 @@
             column.append((re * c + im * w, im * c - re * w))
         for n2, v in enumerate(fft8(column, 1.0)):
             re, im = scaled(v, 2.0 * math.pi * n2 * m1 / 64)
-            re_ref[m1 * 8 + n2] = re
-            im_ref[m1 * 8 + n2] = im
-    for n2 in range(8):
-        column = [(re_ref[m1 * 8 + n2], im_ref[m1 * 8 + n2]) for m1 in range(8)]
-        for n1, (re, im) in enumerate(fft8(column, 1.0)):
-            s = 8 * n1 + n2
-            if s > 0:
-                angle = 2.0 * math.pi * s / 128
-                c = jnp.where(top, 1.0, math.cos(angle))
-                w = jnp.where(top, 0.0, math.sin(angle))
-                re, im = re * c - im * w, im * c + re * w
-            total = jnp.where(top, re, pltpu.roll(im, 4, 0))
-            delta = jnp.where(top, pltpu.roll(re, 4, 0), im)
-            out_ref[s, o] = encode(total + delta)
-            out_ref[s + 64, o] = encode(total - delta)
-
-
-def rows_inverse(o, in_ref, matrix_ref, twist_ref, out_ref, value_ref):
+            re_ref[o, m1 * 8 + n2] = re
+            im_ref[o, m1 * 8 + n2] = im
+
+
+def columns_out(n2, o, pairs_ref, re_ref, im_ref, out_ref):
+    top = lax.broadcasted_iota(jnp.int32, (8, 128), 0) < 4
+    column = [(re_ref[o, m1 * 8 + n2], im_ref[o, m1 * 8 + n2]) for m1 in range(8)]
+    for n1, (re, im) in enumerate(fft8(column, 1.0)):
+        s = 8 * n1 + n2
+        c = jnp.where(top, 1.0, pairs_ref[0, s])
+        w = jnp.where(top, 0.0, pairs_ref[1, s])
+        re, im = re * c - im * w, im * c + re * w
+        total = jnp.where(top, re, pltpu.roll(im, 4, 0))
+        delta = jnp.where(top, pltpu.roll(re, 4, 0), im)
+        out_ref[s, o] = encode(total + delta)
+        out_ref[s + 64, o] = encode(total - delta)
+
+
+def rows_inverse(o, hi_ref, lo_ref, matrix_ref, twist_ref, out_ref, value_ref):
     for h in range(2):
-        hi, lo = split(decode(in_ref[:, h, o]).reshape(512, 128))
+        hi, lo = hi_ref[:, h, o].reshape(512, 128), lo_ref[:, h, o].reshape(512, 128)
         rows = pl.ds(h * 128, 128)
         value_ref[rows, :] = dot3((hi, lo), (matrix_ref[0], matrix_ref[1]), TN)
     for half in range(2):
@@ -372,8 +381,9 @@
 PHASE_ORDER = ((1, 0), (0, 1), (3, 0), (1, 1), (2, 0), (3, 1), (2, 1), (0, 0))
 
 
-def head(i, j, weight_ref, bias_ref, band_ref, tile_ref, sums_ref, sides_ref, edges_ref, got_sides_ref, got_edges_ref, got_corners_ref, phase_ref, down, border_sems, send_phase, meanwhile):
+def head(i, j, weight_ref, bias_ref, band_ref, tile_ref, sums_ref, sides_ref, edges_ref, got_sides_ref, got_edges_ref, got_corners_ref, phase_ref, load, down, border_sems, send_phase, meanwhile):
     band(weight_ref, band_ref)
+    load.wait()
     lane = lax.broadcasted_iota(jnp.int32, (32, 128), 1)
     tall = lax.broadcasted_iota(jnp.int32, (32, 128), 0)
     to_right = jnp.zeros((32, 128), F32)
@@ -457,27 +467,26 @@
 
 
 def spectral_kernel(
-    weight_ref, bias_ref, wave_ref, travel_ref, features_ref,
+    weight_ref, bias_ref, wave_ref, travel_ref, pairs_ref, turns_ref, features_ref,
     forward_hbm, lanes_hbm, back_hbm, twist_x_hbm, twist_y_ref,
-    returned_ref,
+    high_ref, low_ref,
     forward_ref, lanes_ref, back_ref, twist_x_ref,
     tile_ref, band_ref, sums_ref, sides_ref, edges_ref, got_sides_ref, got_edges_ref, got_corners_ref, phase_ref, got_phase_ref,
-    packets_ref, spread_in_ref, filtered_ref, cos_ref, sin_ref, re_ref, im_ref, hi_ref, lo_ref, field_hi_ref, field_lo_ref,
-    tile_sem, table_sems, border_send, border_recv, send_sems, recv_sems, local_sems,
+    packets_ref, spread_in_ref, filtered_ref, returned_ref, cos_ref, sin_ref, re_ref, im_ref, hi_ref, lo_ref, field_hi_ref, field_lo_ref,
+    tile_sem, table_sems, border_send, border_recv, send_sems, recv_sems, local_sems, group_sems,
 ):
     colors = 3
     i, j = lax.axis_index("row"), lax.axis_index("col")
     me = i * 16 + j
-    down = enter(i, j)
     load = pltpu.make_async_copy(features_ref, tile_ref.at[:, pl.ds(16, 256), :], tile_sem)
     load.start()
+    down = enter(i, j)
     tables_in = []
     for n, (source, target) in enumerate(((forward_hbm, forward_ref), (lanes_hbm, lanes_ref), (back_hbm, back_ref), (twist_x_hbm, twist_x_ref))):
         tables_in.append(pltpu.make_async_copy(source, target, table_sems.at[n]))
         tables_in[n].start()
     tile_ref[:, 0:16, :] = jnp.zeros((16, 16, 256), BF16)
     tile_ref[:, 272:288, :] = jnp.zeros((16, 16, 256), BF16)
-    load.wait()
 
     def each(body):
         def step(o, carry):
@@ -502,12 +511,10 @@
 
     head(
         i, j, weight_ref, bias_ref, band_ref, tile_ref, sums_ref, sides_ref, edges_ref, got_sides_ref, got_edges_ref, got_corners_ref, phase_ref,
-        down, (border_send, border_recv), send_phase,
+        load, down, (border_send, border_recv), send_phase,
         lambda: each(lambda o: transfer(o, me, wave_ref[o], travel_ref[0], cos_ref, sin_ref)),
     )
 
-    first = (send_sems.at[0], recv_sems.at[0], local_sems.at[0])
-    second = (send_sems.at[1], recv_sems.at[1], local_sems.at[1])
     by_pair = packets_ref.reshape(64, 2, colors, 8, 128)
 
     def forward(o):
@@ -516,21 +523,59 @@
 
     tables_in[0].wait()
     each(forward)
-    send_all(me, lambda d: packets_ref.at[d], spread_in_ref, *first)
+
+    def groups(body):
+        def step(c, carry):
+            body(c)
+            return carry
+
+        lax.fori_loop(0, 8, step, 0)
+
+    groups(lambda c: send_group(c, me, packets_ref, spread_in_ref, send_sems.at[0], group_sems.at[c], local_sems.at[0]))
+
+    def wait_group(c, landing, local_sem, sem):
+        @pl.when(c == 0)
+        def _():
+            wait_for(landing.at[0], local_sem)
+            wait_for(landing.at[pl.ds(0, 15)], sem)
+
+        @pl.when(c != 0)
+        def _():
+            wait_for(landing.at[pl.ds(0, 16)], sem)
+
+    def arrive(c):
+        wait_group(c, spread_in_ref, local_sems.at[0], group_sems.at[c])
+        for o in range(colors):
+            columns_in((me - c + 8) % 8, o, spread_in_ref, pairs_ref, turns_ref, re_ref, im_ref)
+
+    def leave(c):
+        for o in range(colors):
+            columns_out((me + c) % 8, o, pairs_ref, re_ref, im_ref, filtered_ref)
+        send_group(c, me, filtered_ref, returned_ref, send_sems.at[1], group_sems.at[8 + c], local_sems.at[1])
+
+    groups(arrive)
     for table in tables_in[1:]:
         table.wait()
-    wait_all(spread_in_ref, *first)
-    each(lambda o: columns(o, spread_in_ref, lanes_ref, back_ref, twist_x_ref, cos_ref, sin_ref, filtered_ref, re_ref, im_ref, hi_ref, lo_ref))
-    send_all(me, lambda d: filtered_ref.at[d], returned_ref, *second)
-    wait_all(returned_ref, *second)
-
-
-def rows_inverse_kernel(returned_ref, matrix_ref, twist_ref, out_ref, value_ref, result_ref, sems):
+    each(lambda o: columns(o, lanes_ref, back_ref, twist_x_ref, cos_ref, sin_ref, re_ref, im_ref, hi_ref, lo_ref))
+    groups(leave)
+    wait_for(packets_ref.at[pl.ds(0, 127)], send_sems.at[0])
+
+    def finish(c):
+        wait_group(c, returned_ref, local_sems.at[1], group_sems.at[8 + c])
+        for m in range(16):
+            d = (me - c + 8 * m + 8) % 128
+            high_ref[d], low_ref[d] = split(decode(returned_ref[d]))
+
+    groups(finish)
+    wait_for(filtered_ref.at[pl.ds(0, 127)], send_sems.at[1])
+
+
+def rows_inverse_kernel(hi_ref, lo_ref, matrix_ref, twist_ref, out_ref, value_ref, result_ref, sems):
     colors = result_ref.shape[0]
-    by_pair = returned_ref.reshape(64, 2, colors, 8, 128)
+    by_pair = [ref.reshape(64, 2, colors, 8, 128) for ref in (hi_ref, lo_ref)]
 
     def step(o, carry):
-        rows_inverse(o, by_pair, matrix_ref, twist_ref, result_ref, value_ref)
+        rows_inverse(o, *by_pair, matrix_ref, twist_ref, result_ref, value_ref)
         pltpu.make_async_copy(result_ref.at[o], out_ref.at[o], sems.at[o]).start()
         return carry
 
@@ -547,11 +592,11 @@
     smem = pl.BlockSpec(memory_space=pltpu.SMEM)
     vmem = pl.BlockSpec(memory_space=pltpu.VMEM)
     exchange = pltpu.VMEM((128, colors, 8, 128), BF16)
-    returned = pl.pallas_call(
+    high, low = pl.pallas_call(
         spectral_kernel,
-        in_specs=[vmem] + [smem] * 3 + [pl.BlockSpec(memory_space=pl.ANY)] * 5 + [vmem],
-        out_specs=vmem,
-        out_shape=pltpu.VMEM((128, colors, 8, 128), BF16),
+        in_specs=[vmem] + [smem] * 5 + [pl.BlockSpec(memory_space=pl.ANY)] * 5 + [vmem],
+        out_specs=[vmem] * 2,
+        out_shape=[pltpu.VMEM((128, colors, 8, 128), BF16)] * 2,
         scratch_shapes=[
             *(pltpu.VMEM(a.shape, a.dtype) for a in args[:4]),
             pltpu.VMEM((16, 288, 256), BF16),
@@ -564,11 +609,11 @@
             pltpu.VMEM((4, 8, 128), F32),
             pltpu.VMEM((colors, 16, 16, 256), BF16),
             pltpu.VMEM((colors, 16, 16, 256), BF16),
-            exchange, exchange, exchange,
+            exchange, exchange, exchange, exchange,
             pltpu.VMEM((colors, 64, 8, 128), F32),
             pltpu.VMEM((colors, 64, 8, 128), F32),
-            pltpu.VMEM((64, 8, 128), F32),
-            pltpu.VMEM((64, 8, 128), F32),
+            pltpu.VMEM((colors, 64, 8, 128), F32),
+            pltpu.VMEM((colors, 64, 8, 128), F32),
             pltpu.VMEM((64, 8, 256), BF16),
             pltpu.VMEM((64, 8, 256), BF16),
             pltpu.VMEM((256, 512), BF16),
@@ -580,13 +625,14 @@
             pltpu.SemaphoreType.DMA((5,)),
             pltpu.SemaphoreType.DMA((5,)),
             pltpu.SemaphoreType.DMA((5,)),
+            pltpu.SemaphoreType.DMA((16,)),
         ],
         compiler_params=pltpu.CompilerParams(collective_id=0, has_side_effects=True, vmem_limit_bytes=VMEM_LIMIT),
         name="spectral",
-    )(conv_weight.transpose(0, 2, 3, 1), bias, wave, travel, features, *args)
+    )(conv_weight.transpose(0, 2, 3, 1), bias, wave, travel, jnp.asarray(table["pairs"]), jnp.asarray(table["turns"]), features, *args)
     return pl.pallas_call(
         rows_inverse_kernel,
-        in_specs=[vmem] * 3,
+        in_specs=[vmem] * 4,
         out_specs=pl.BlockSpec(memory_space=pl.ANY),
         out_shape=jax.ShapeDtypeStruct((colors, 2, 16, 4096), BF16),
         scratch_shapes=[
@@ -596,7 +642,7 @@
         ],
         compiler_params=pltpu.CompilerParams(vmem_limit_bytes=16 * 1024 * 1024),
         name="rows_inverse",
-    )(returned, args[0], args[4])
+    )(high, low, args[0], args[4])
 
 
 def solution(mesh):

time: 59.3 us -> 57.9 us (0.976)
  Pallas kernels: 58.4 us -> 57 us
    pallas_call x2, Pallas kernels: 58.4 us -> 57 us  [the longest x1 54.1 us: per_device(): pl.pallas_call(spectral_kernel, in_specs=[vmem] + [smem] * 5 + [pl.BlockS...]
where the time goes in v6:
time: 57.9 us; the launch traced here: 57.7 us
  Pallas kernels  57 us (98%)
  between operations  0.69 us (1%)
    pallas_call x1, Pallas kernels, per_device(): pl.pallas_call(spectral_kernel, in_specs=[vmem] + [smem] * 5 + [pl.BlockS...  54.1 us
    pallas_call x1, Pallas kernels, per_device(): pl.pallas_call(rows_inverse_kernel, in_specs=[vmem] * 4, out_specs=pl.Blo...  2.96 us

profile of v6, /device:TPU:1, one launch (start us, length us, event | category | flops | bytes accessed | tf_op | source)
XLA Modules:
  0.0 57.7 jit_solution(15022383047563703316)
XLA Ops:
  0.7 0.0 copy-start
  0.7 0.0 copy-start.1
  0.7 54.1 %spectral.1 = (bf16[128,3,8,128]{3,2,1,0:T(8,128)(2,1)S(1)}, bf16[128,3,8,128]{3,2,1,0:T(8,128)(2,1)S(1)}) custom-call(bf16[3,3,3,16]{3,2,1,0:T(4,128)(2,1)} %bitcast.1, f32[3]{0:T(128)} %bias_ref.1, f32[3]{0:T(128)} %wave_ref.1, f32[1]{0:T(128)S(6)} %copy.13.travel_ref, f32[2,64]{1,0:T(2,128)} %constant.19.clone.pairs_ref, ...), custom_call_target="tpu_custom_call" | custom-call | tf_op jit(solution)/shard_map/spectral/pallas_call | solution.py:595
  54.8 0.0 copy-done
  54.8 0.0 copy-done.1
  54.8 3.0 %rows_inverse.1 = bf16[3,2,16,4096]{3,2,1,0:T(8,128)(2,1)} custom-call(bf16[128,3,8,128]{3,2,1,0:T(8,128)(2,1)S(1)} %get-tuple-element.7.hi_ref, bf16[128,3,8,128]{3,2,1,0:T(8,128)(2,1)S(1)} %get-tuple-element.8.lo_ref, bf16[2,512,512]{2,1,0:T(8,128)(2,1)S(1)} %copy-done, f32[2,16,256]{2,1,0:T(8,128)S(1)} %copy-done.1), custom_call_target="tpu_custom_call" | custom-call | tf_op jit(solution)/shard_map/rows_inverse/pallas_call | solution.py:633
Async XLA Ops:
  0.7 54.1 %copy-start = (bf16[2,512,512]{2,1,0:T(8,128)(2,1)S(1)}, bf16[2,512,512]{2,1,0:T(8,128)(2,1)}, u32[]{:S(2)}) copy-start(bf16[2,512,512]{2,1,0:T(8,128)(2,1)} %constant.14.clone.forward_hbm.matrix_ref) | copy-start | bytes 3145732
  0.7 54.1 %copy-start.1 = (f32[2,16,256]{2,1,0:T(8,128)S(1)}, f32[2,16,256]{2,1,0:T(8,128)}, u32[]{:S(2)}) copy-start(f32[2,16,256]{2,1,0:T(8,128)} %constant.18.clone.twist_y_ref.twist_ref) | copy-start | bytes 98308

commit v7 on v6

--- a/solution.py
+++ b/solution.py
@@ -25,16 +25,16 @@
 
 
 def tables():
-    k2 = np.arange(256)
     b = np.arange(256)
-    rot = rotation_np(2.0 * np.pi * ((k2[:, None] * b[None, :]) % 256) / 256.0)
-    forward_y = rot.reshape(2, 2, 64, 4, 256).transpose(2, 0, 3, 1, 4).reshape(512, 512)
+    m = np.arange(128)
+    rot = rotation_np(2.0 * np.pi * ((m[:, None] * m[None, :]) % 128) / 128.0)
+    forward_y = rot.reshape(2, 2, 32, 4, 128).transpose(2, 0, 3, 1, 4).reshape(256, 256)
     j = np.arange(16)
     rot16 = rotation_np(2.0 * np.pi * ((j[:, None] * j[None, :]) % 16) / 16.0)
     back16 = np.stack([np.stack([rot16[0, 0], -rot16[0, 1]]), np.stack([-rot16[1, 0], rot16[1, 1]])])
     lanes = np.einsum("pqab,cd->qcbpda", rot16, np.eye(8)).reshape(256, 256)
     lanes_back = np.einsum("pqab,cd->qcbpda", back16, np.eye(8)).reshape(256, 256)
-    k1 = np.arange(16)
+    k1 = np.minimum(np.arange(24), 16)
     angle = 2.0 * np.pi * ((k1[:, None] * b[None, :]) % 4096) / 4096.0
     twist_y = np.stack([np.cos(angle), -np.sin(angle)]).astype(np.float32)
     p = np.arange(128).reshape(64, 2)
@@ -210,7 +210,8 @@
     wait_for(others, recv_sem)
 
 
-def rows_forward(o, phase_ref, matrix_ref, twist_ref, out_ref, hi_ref, lo_ref):
+def rows_forward(o, phase_ref, matrix_ref, twist_ref, out_ref, half_ref, hi_ref, lo_ref):
+    step_c, step_s = twist_ref[0, 16:17, :128], twist_ref[1, 16:17, :128]
     for half in range(2):
         cols = pl.ds(half * 128, 128)
         field = []
@@ -224,21 +225,34 @@
                 s = twist_ref[1, pl.ds(k1, 1), cols]
                 re, im = re * c - im * s, re * s + im * c
             rows = pl.ds(k1 * 16, 16)
-            for part, value in enumerate((re, im)):
-                hi, lo = split(value)
-                place = pl.ds(part * 256 + half * 128, 128)
-                hi_ref[rows, place] = hi
-                lo_ref[rows, place] = lo
-    result = dot3((matrix_ref[0], matrix_ref[1]), (hi_ref[...], lo_ref[...]), NT)
-    for h in range(2):
-        out_ref[:, h, o] = encode(result[:, h * 128 : (h + 1) * 128]).reshape(64, 8, 128)
+            if half == 0:
+                half_ref[0, rows, :] = re
+                half_ref[1, rows, :] = im
+                continue
+            low_re, low_im = half_ref[0, rows, :], half_ref[1, rows, :]
+            dre, dim = low_re - re, low_im - im
+            even = (low_re + re, low_im + im)
+            odd = (dre * step_c - dim * step_s, dre * step_s + dim * step_c)
+            for parity, values in enumerate((even, odd)):
+                rows = pl.ds(parity * 256 + k1 * 16, 16)
+                for part, value in enumerate(values):
+                    hi, lo = split(value)
+                    place = pl.ds(part * 128, 128)
+                    hi_ref[rows, place] = hi
+                    lo_ref[rows, place] = lo
+    for parity in range(2):
+        rows = pl.ds(parity * 256, 256)
+        result = dot3((matrix_ref[0], matrix_ref[1]), (hi_ref[rows, :], lo_ref[rows, :]), NT)
+        for h in range(2):
+            out_ref[pl.ds(parity * 32, 32), h, o] = encode(result[:, h * 128 : (h + 1) * 128]).reshape(32, 8, 128)
 
 
 def transfer(o, me, wave, travel, cos_ref, sin_ref):
     row = lax.broadcasted_iota(jnp.int32, (8, 128), 0)
     lane = lax.broadcasted_iota(jnp.int32, (8, 128), 1)
     base_x = (row // 4) + 128 * (lane % 16)
-    freq_y = 8 * (me % 2) + lane // 16 + 16 * (4 * (me // 2) + row % 4)
+    group = me // 2
+    freq_y = 8 * (me % 2) + lane // 16 + 16 * (2 * (4 * (group % 32) + row % 4) + group // 32)
     signed_y = jnp.where(freq_y < 2048, freq_y, freq_y - 4096).astype(F32) * (1.0 / 4096)
     square_y = signed_y * signed_y
 
@@ -326,10 +340,18 @@
 
 
 def rows_inverse(o, hi_ref, lo_ref, matrix_ref, twist_ref, out_ref, value_ref):
+    step_c, step_s = twist_ref[0, 16:17, :128], twist_ref[1, 16:17, :128]
     for h in range(2):
         hi, lo = hi_ref[:, h, o].reshape(512, 128), lo_ref[:, h, o].reshape(512, 128)
         rows = pl.ds(h * 128, 128)
-        value_ref[rows, :] = dot3((hi, lo), (matrix_ref[0], matrix_ref[1]), TN)
+        even = dot3((hi[:256], lo[:256]), (matrix_ref[0], matrix_ref[1]), TN)
+        odd = dot3((hi[256:], lo[256:]), (matrix_ref[0], matrix_ref[1]), TN)
+        re, im = odd[:, :128], odd[:, 128:]
+        re, im = re * step_c + im * step_s, im * step_c - re * step_s
+        value_ref[rows, 0:128] = even[:, :128] + re
+        value_ref[rows, 128:256] = even[:, :128] - re
+        value_ref[rows, 256:384] = even[:, 128:] + im
+        value_ref[rows, 384:512] = even[:, 128:] - im
     for half in range(2):
         cols = pl.ds(half * 128, 128)
         spectrum = []
@@ -472,7 +494,7 @@
     high_ref, low_ref,
     forward_ref, lanes_ref, back_ref, twist_x_ref,
     tile_ref, band_ref, sums_ref, sides_ref, edges_ref, got_sides_ref, got_edges_ref, got_corners_ref, phase_ref, got_phase_ref,
-    packets_ref, spread_in_ref, filtered_ref, returned_ref, cos_ref, sin_ref, re_ref, im_ref, hi_ref, lo_ref, field_hi_ref, field_lo_ref,
+    packets_ref, spread_in_ref, filtered_ref, returned_ref, cos_ref, sin_ref, re_ref, im_ref, hi_ref, lo_ref, half_ref, field_hi_ref, field_lo_ref,
     tile_sem, table_sems, border_send, border_recv, send_sems, recv_sems, local_sems, group_sems,
 ):
     colors = 3
@@ -519,7 +541,7 @@
 
     def forward(o):
         wait_all(got_phase_ref.at[o], send_sems.at[2 + o], recv_sems.at[2 + o], local_sems.at[2 + o])
-        rows_forward(o, got_phase_ref, forward_ref, twist_y_ref, by_pair, field_hi_ref, field_lo_ref)
+        rows_forward(o, got_phase_ref, forward_ref, twist_y_ref, by_pair, half_ref, field_hi_ref, field_lo_ref)
 
     tables_in[0].wait()
     each(forward)
@@ -616,8 +638,9 @@
             pltpu.VMEM((colors, 64, 8, 128), F32),
             pltpu.VMEM((64, 8, 256), BF16),
             pltpu.VMEM((64, 8, 256), BF16),
-            pltpu.VMEM((256, 512), BF16),
-            pltpu.VMEM((256, 512), BF16),
+            pltpu.VMEM((2, 256, 128), F32),
+            pltpu.VMEM((512, 256), BF16),
+            pltpu.VMEM((512, 256), BF16),
             pltpu.SemaphoreType.DMA,
             pltpu.SemaphoreType.DMA((4,)),
             pltpu.SemaphoreType.DMA((8,)),

time: 57.9 us -> 57.1 us (0.986)
  Pallas kernels: 57 us -> 56.2 us
where the time goes in v7:
time: 57.1 us; the launch traced here: 56.9 us
  Pallas kernels  56.2 us (98%)
  between operations  0.72 us (1%)
    pallas_call x1, Pallas kernels, per_device(): pl.pallas_call(spectral_kernel, in_specs=[vmem] + [smem] * 5 + [pl.BlockS...  53.8 us
    pallas_call x1, Pallas kernels, per_device(): pl.pallas_call(rows_inverse_kernel, in_specs=[vmem] * 4, out_specs=pl.Blo...  2.39 us

profile of v7, /device:TPU:1, one launch (start us, length us, event | category | flops | bytes accessed | tf_op | source)
XLA Modules:
  0.0 56.9 jit_solution(13477156031258747267)
XLA Ops:
  0.0 0.0 copy-start.1
  0.0 0.0 copy-start
  0.7 53.8 %spectral.1 = (bf16[128,3,8,128]{3,2,1,0:T(8,128)(2,1)S(1)}, bf16[128,3,8,128]{3,2,1,0:T(8,128)(2,1)S(1)}) custom-call(bf16[3,3,3,16]{3,2,1,0:T(4,128)(2,1)} %bitcast.1, f32[3]{0:T(128)} %bias_ref.1, f32[3]{0:T(128)} %wave_ref.1, f32[1]{0:T(128)S(6)} %copy.13.travel_ref, f32[2,64]{1,0:T(2,128)} %constant.19.clone.pairs_ref, ...), custom_call_target="tpu_custom_call" | custom-call | tf_op jit(solution)/shard_map/spectral/pallas_call | solution.py:617
  54.5 0.0 copy-done.1
  54.5 0.0 copy-done
  54.5 2.4 %rows_inverse.1 = bf16[3,2,16,4096]{3,2,1,0:T(8,128)(2,1)} custom-call(bf16[128,3,8,128]{3,2,1,0:T(8,128)(2,1)S(1)} %get-tuple-element.7.hi_ref, bf16[128,3,8,128]{3,2,1,0:T(8,128)(2,1)S(1)} %get-tuple-element.8.lo_ref, bf16[2,256,256]{2,1,0:T(8,128)(2,1)S(1)} %copy-done, f32[2,24,256]{2,1,0:T(8,128)S(1)} %copy-done.1), custom_call_target="tpu_custom_call" | custom-call | tf_op jit(solution)/shard_map/rows_inverse/pallas_call | solution.py:656
Async XLA Ops:
  0.0 54.5 %copy-start.1 = (f32[2,24,256]{2,1,0:T(8,128)S(1)}, f32[2,24,256]{2,1,0:T(8,128)}, u32[]{:S(2)}) copy-start(f32[2,24,256]{2,1,0:T(8,128)} %constant.18.clone.twist_y_ref.twist_ref) | copy-start | bytes 147460
  0.0 54.5 %copy-start = (bf16[2,256,256]{2,1,0:T(8,128)(2,1)S(1)}, bf16[2,256,256]{2,1,0:T(8,128)(2,1)}, u32[]{:S(2)}) copy-start(bf16[2,256,256]{2,1,0:T(8,128)(2,1)} %constant.14.clone.forward_hbm.matrix_ref) | copy-start | bytes 786436

commit v8 on v7

--- a/solution.py
+++ b/solution.py
@@ -405,12 +405,14 @@
 
 def head(i, j, weight_ref, bias_ref, band_ref, tile_ref, sums_ref, sides_ref, edges_ref, got_sides_ref, got_edges_ref, got_corners_ref, phase_ref, load, down, border_sems, send_phase, meanwhile):
     band(weight_ref, band_ref)
-    load.wait()
+    load[0].wait()
     lane = lax.broadcasted_iota(jnp.int32, (32, 128), 1)
     tall = lax.broadcasted_iota(jnp.int32, (32, 128), 0)
     to_right = jnp.zeros((32, 128), F32)
     to_left = jnp.zeros((32, 128), F32)
     for k in range(8):
+        if k == 3:
+            load[1].wait()
         window = tile_ref[:, k * 32 : k * 32 + 64, :].reshape(1024, 256)
         count = 320 if k in (0, 7) else 288
         value = jnp.dot(band_ref[:count], window, preferred_element_type=F32)
@@ -472,7 +474,7 @@
 
         def block(k):
             index = 3 * k + o
-            before = pltpu.roll(got_sides_ref[0], 128 - index, 1)
+            before = pltpu.roll(got_sides_ref[0], (128 - index) % 128, 1)
             after = pltpu.roll(got_sides_ref[1], 127 - index, 1)
             first = pltpu.roll(sums_ref[k, o], 1, 1)
             last = pltpu.roll(sums_ref[k, 6 + o], 255, 1)
@@ -500,8 +502,12 @@
     colors = 3
     i, j = lax.axis_index("row"), lax.axis_index("col")
     me = i * 16 + j
-    load = pltpu.make_async_copy(features_ref, tile_ref.at[:, pl.ds(16, 256), :], tile_sem)
-    load.start()
+    load = [
+        pltpu.make_async_copy(features_ref.at[:, pl.ds(128 * n, 128), :], tile_ref.at[:, pl.ds(16 + 128 * n, 128), :], tile_sem.at[n])
+        for n in range(2)
+    ]
+    for part in load:
+        part.start()
     down = enter(i, j)
     tables_in = []
     for n, (source, target) in enumerate(((forward_hbm, forward_ref), (lanes_hbm, lanes_ref), (back_hbm, back_ref), (twist_x_hbm, twist_x_ref))):
@@ -641,7 +647,7 @@
             pltpu.VMEM((2, 256, 128), F32),
             pltpu.VMEM((512, 256), BF16),
             pltpu.VMEM((512, 256), BF16),
-            pltpu.SemaphoreType.DMA,
+            pltpu.SemaphoreType.DMA((2,)),
             pltpu.SemaphoreType.DMA((4,)),
             pltpu.SemaphoreType.DMA((8,)),
             pltpu.SemaphoreType.DMA((8,)),

time: 57.1 us -> 57.2 us (level)
  no operation moved by 1% of the time
where the time goes in v8:
time: 57.2 us; the launch traced here: 57 us
  Pallas kernels  56.3 us (98%)
  between operations  0.72 us (1%)
    pallas_call x1, Pallas kernels, per_device(): pl.pallas_call(spectral_kernel, in_specs=[vmem] + [smem] * 5 + [pl.BlockS...  53.9 us
    pallas_call x1, Pallas kernels, per_device(): pl.pallas_call(rows_inverse_kernel, in_specs=[vmem] * 4, out_specs=pl.Blo...  2.39 us

profile of v8, /device:TPU:1, one launch (start us, length us, event | category | flops | bytes accessed | tf_op | source)
XLA Modules:
  0.0 57.0 jit_solution(12655119955661864985)
XLA Ops:
  0.0 0.0 copy-start.1
  0.0 0.0 copy-start
  0.7 53.9 %spectral.1 = (bf16[128,3,8,128]{3,2,1,0:T(8,128)(2,1)S(1)}, bf16[128,3,8,128]{3,2,1,0:T(8,128)(2,1)S(1)}) custom-call(bf16[3,3,3,16]{3,2,1,0:T(4,128)(2,1)} %bitcast.1, f32[3]{0:T(128)} %bias_ref.1, f32[3]{0:T(128)} %wave_ref.1, f32[1]{0:T(128)S(6)} %copy.13.travel_ref, f32[2,64]{1,0:T(2,128)} %constant.19.clone.pairs_ref, ...), custom_call_target="tpu_custom_call" | custom-call | tf_op jit(solution)/shard_map/spectral/pallas_call | solution.py:623
  54.6 0.0 copy-done.1
  54.6 0.0 copy-done
  54.6 2.4 %rows_inverse.1 = bf16[3,2,16,4096]{3,2,1,0:T(8,128)(2,1)} custom-call(bf16[128,3,8,128]{3,2,1,0:T(8,128)(2,1)S(1)} %get-tuple-element.7.hi_ref, bf16[128,3,8,128]{3,2,1,0:T(8,128)(2,1)S(1)} %get-tuple-element.8.lo_ref, bf16[2,256,256]{2,1,0:T(8,128)(2,1)S(1)} %copy-done, f32[2,24,256]{2,1,0:T(8,128)S(1)} %copy-done.1), custom_call_target="tpu_custom_call" | custom-call | tf_op jit(solution)/shard_map/rows_inverse/pallas_call | solution.py:662
Async XLA Ops:
  0.0 54.6 %copy-start.1 = (f32[2,24,256]{2,1,0:T(8,128)S(1)}, f32[2,24,256]{2,1,0:T(8,128)}, u32[]{:S(2)}) copy-start(f32[2,24,256]{2,1,0:T(8,128)} %constant.18.clone.twist_y_ref.twist_ref) | copy-start | bytes 147460
  0.0 54.6 %copy-start = (bf16[2,256,256]{2,1,0:T(8,128)(2,1)S(1)}, bf16[2,256,256]{2,1,0:T(8,128)(2,1)}, u32[]{:S(2)}) copy-start(bf16[2,256,256]{2,1,0:T(8,128)(2,1)} %constant.14.clone.forward_hbm.matrix_ref) | copy-start | bytes 786436

commit v9 on v8

--- a/solution.py
+++ b/solution.py
@@ -584,7 +584,8 @@
     groups(arrive)
     for table in tables_in[1:]:
         table.wait()
-    each(lambda o: columns(o, lanes_ref, back_ref, twist_x_ref, cos_ref, sin_ref, re_ref, im_ref, hi_ref, lo_ref))
+    for o in range(colors):
+        columns(o, lanes_ref, back_ref, twist_x_ref, cos_ref, sin_ref, re_ref, im_ref, hi_ref.at[o], lo_ref.at[o])
     groups(leave)
     wait_for(packets_ref.at[pl.ds(0, 127)], send_sems.at[0])
 
@@ -602,12 +603,9 @@
     colors = result_ref.shape[0]
     by_pair = [ref.reshape(64, 2, colors, 8, 128) for ref in (hi_ref, lo_ref)]
 
-    def step(o, carry):
-        rows_inverse(o, *by_pair, matrix_ref, twist_ref, result_ref, value_ref)
+    for o in range(colors):
+        rows_inverse(o, *by_pair, matrix_ref, twist_ref, result_ref, value_ref.at[o])
         pltpu.make_async_copy(result_ref.at[o], out_ref.at[o], sems.at[o]).start()
-        return carry
-
-    lax.fori_loop(0, colors, step, 0)
     for o in range(colors):
         pltpu.make_async_copy(result_ref.at[o], out_ref.at[o], sems.at[o]).wait()
 
@@ -642,8 +640,8 @@
             pltpu.VMEM((colors, 64, 8, 128), F32),
             pltpu.VMEM((colors, 64, 8, 128), F32),
             pltpu.VMEM((colors, 64, 8, 128), F32),
-            pltpu.VMEM((64, 8, 256), BF16),
-            pltpu.VMEM((64, 8, 256), BF16),
+            pltpu.VMEM((colors, 64, 8, 256), BF16),
+            pltpu.VMEM((colors, 64, 8, 256), BF16),
             pltpu.VMEM((2, 256, 128), F32),
             pltpu.VMEM((512, 256), BF16),
             pltpu.VMEM((512, 256), BF16),
@@ -665,7 +663,7 @@
         out_specs=pl.BlockSpec(memory_space=pl.ANY),
         out_shape=jax.ShapeDtypeStruct((colors, 2, 16, 4096), BF16),
         scratch_shapes=[
-            pltpu.VMEM((256, 512), F32),
+            pltpu.VMEM((colors, 256, 512), F32),
             pltpu.VMEM((colors, 2, 16, 4096), BF16),
             pltpu.SemaphoreType.DMA((colors,)),
         ],

time: 57.2 us -> 56 us (0.979)
  Pallas kernels: 56.3 us -> 55.1 us
    pallas_call x1, Pallas kernels: 53.9 us -> 53.2 us  [per_device(): pl.pallas_call(spectral_kernel, in_specs=[vmem] + [smem] * 5 + [pl.BlockS...]
where the time goes in v9:
time: 56 us; the launch traced here: 55.8 us
  Pallas kernels  55.1 us (98%)
  between operations  0.72 us (1%)
    pallas_call x1, Pallas kernels, per_device(): pl.pallas_call(spectral_kernel, in_specs=[vmem] + [smem] * 5 + [pl.BlockS...  53.2 us
    pallas_call x1, Pallas kernels, per_device(): pl.pallas_call(rows_inverse_kernel, in_specs=[vmem] * 4, out_specs=pl.Blo...  1.92 us

profile of v9, /device:TPU:1, one launch (start us, length us, event | category | flops | bytes accessed | tf_op | source)
XLA Modules:
  0.0 55.8 jit_solution(17622327776903465458)
XLA Ops:
  0.0 0.0 copy-start.1
  0.0 0.0 copy-start
  0.7 53.2 %spectral.1 = (bf16[128,3,8,128]{3,2,1,0:T(8,128)(2,1)S(1)}, bf16[128,3,8,128]{3,2,1,0:T(8,128)(2,1)S(1)}) custom-call(bf16[3,3,3,16]{3,2,1,0:T(4,128)(2,1)} %bitcast.1, f32[3]{0:T(128)} %bias_ref.1, f32[3]{0:T(128)} %wave_ref.1, f32[1]{0:T(128)S(6)} %copy.13.travel_ref, f32[2,64]{1,0:T(2,128)} %constant.19.clone.pairs_ref, ...), custom_call_target="tpu_custom_call" | custom-call | tf_op jit(solution)/shard_map/spectral/pallas_call | solution.py:621
  53.9 0.0 copy-done.1
  53.9 0.0 copy-done
  53.9 1.9 %rows_inverse.1 = bf16[3,2,16,4096]{3,2,1,0:T(8,128)(2,1)} custom-call(bf16[128,3,8,128]{3,2,1,0:T(8,128)(2,1)S(1)} %get-tuple-element.7.hi_ref, bf16[128,3,8,128]{3,2,1,0:T(8,128)(2,1)S(1)} %get-tuple-element.8.lo_ref, bf16[2,256,256]{2,1,0:T(8,128)(2,1)S(1)} %copy-done, f32[2,24,256]{2,1,0:T(8,128)S(1)} %copy-done.1), custom_call_target="tpu_custom_call" | custom-call | tf_op jit(solution)/shard_map/rows_inverse/pallas_call | solution.py:660
Async XLA Ops:
  0.0 53.9 %copy-start.1 = (f32[2,24,256]{2,1,0:T(8,128)S(1)}, f32[2,24,256]{2,1,0:T(8,128)}, u32[]{:S(2)}) copy-start(f32[2,24,256]{2,1,0:T(8,128)} %constant.18.clone.twist_y_ref.twist_ref) | copy-start | bytes 147460
  0.0 53.9 %copy-start = (bf16[2,256,256]{2,1,0:T(8,128)(2,1)S(1)}, bf16[2,256,256]{2,1,0:T(8,128)(2,1)}, u32[]{:S(2)}) copy-start(bf16[2,256,256]{2,1,0:T(8,128)(2,1)} %constant.14.clone.forward_hbm.matrix_ref) | copy-start | bytes 786436
